TPU v7x, 32 devices: a whole 2x2x4 slice. The times are simulated.
32 devices in a mesh: tok: 8 (over z, x), feat: 4 (over y, core).
Axes of the slice: x: 2, y: 2, z: 4, core: 2. Of those that a mesh axis runs over, the one named last changes fastest.
Arguments:
- activations: bfloat16 [8192, 28672], P('tok', 'feat'), may hold values from -6 to 6
- out_grads: bfloat16 [8192, 8192], P('tok', 'feat'), may hold values from -6 to 6
- proj_in: bfloat16 [28672, 256], P('feat'), may hold values from -0.03125 to 0.03125
- proj_out: bfloat16 [8192, 256], P('feat'), may hold values from -0.0625 to 0.0625
- left_factor: float32 [256, 256], replicated, may hold values from -0.375 to 0.375
- right_factor: float32 [256, 256], replicated, may hold values from -0.375 to 0.375
- seq_lengths: int32 [64], replicated, may hold values from 1 to 255, as said below
- seq_slots: int32 [64], replicated, may hold values from 0 to 63, each once
- stored_grads: float32 [256, 65536], P('tok', 'feat'), may hold values from -0.375 to 0.375
Outputs:
- scores: float32 [256, 64], P(('tok', 'feat'))
- seq_grads: float32 [64, 65536], P('tok', 'feat')
Inputs may be any that keep to these rules, and one draw needn't show every extreme that they name: `seq_lengths`: the lengths sum to 8192. Sequence s starts within tokens s * (128) to (s + 1) * 128 - 1, the first at token 0, so exactly 8 sequences start in the tokens of each index of tok, at most 9 sequences meet them (exactly that many at index 1), and a sequence meets the tokens of at most two indices. The longest is exactly 255. `seq_slots`: every slot is used by exactly one sequence.
All inputs are finite; a program needn't handle non-finite values.
Results may differ from a plain program's by a relative error of at most 0.0003.
Values sent between devices are 32-bit elements; how exact they have to be, the bound alone decides.
A program may use at most 128 MiB of HBM per device.

v0:
```python
import functools

import jax
import jax.numpy as jnp
from jax import lax
from jax.experimental import pallas as pl
from jax.experimental.pallas import tpu as pltpu
from jax.sharding import PartitionSpec as P

MESH = pl.DeviceIdType.MESH
VMEM = pl.BlockSpec(memory_space=pltpu.VMEM)


def remote(src, dst, send_sem, recv_sem, tok, feat):
    return pltpu.make_async_remote_copy(
        src_ref=src, dst_ref=dst, send_sem=send_sem, recv_sem=recv_sem,
        device_id=(tok, feat), device_id_type=MESH,
    )


def greet(barrier, tok, feat):
    pl.semaphore_signal(barrier, inc=1, device_id=(tok, feat), device_id_type=MESH)


def project_kernel(sizes, *refs):
    chips, rows, group_toks, early = sizes
    rows_in, mats_in, stored = refs[0:2], refs[2:4], refs[4]
    outs, traded = refs[5:7], refs[7 : 7 + early]
    refs = refs[7 + early :]
    lhs, rhs, parts, first, held, second = (refs[2 * n : 2 * n + 2] for n in range(6))
    load, send1, recv1, send2, recv2, tsend, trecv = refs[12:]
    tok, feat = lax.axis_index("tok"), lax.axis_index("feat")
    spot = tok % group_toks
    pair, core = feat // 2, feat % 2
    mate = pair * 2 + (1 - core)
    both = 2 * rows
    order = list(range(1, chips)) + [0]

    def lines(step):
        return pl.ds(pl.multiple_of(((pair + step) % chips) * both, both), both)

    loads = {}
    for step in order:
        for k in range(2):
            if step == order[0]:
                loads[k] = pltpu.make_async_copy(mats_in[k], rhs[k], load.at[k, chips])
                loads[k].start()
            loads[k, step] = pltpu.make_async_copy(
                rows_in[k].at[lines(step)], lhs[k].at[step], load.at[k, step]
            )
            loads[k, step].start()

    barrier = pltpu.get_barrier_semaphore()
    greet(barrier, tok, mate)
    for step in range(1, chips):
        greet(barrier, tok, ((pair + step) % chips) * 2 + core)
    for step in range(1, group_toks):
        greet(barrier, tok - spot + (spot + step) % group_toks, feat)
    pl.semaphore_wait(barrier, chips + group_toks - 1)

    wide = traded[0].shape[1]
    trades = []
    for step in range(1, early + 1):
        to = (spot + step) % group_toks
        trades.append(remote(
            stored.at[:, pl.ds(pl.multiple_of(to * wide, wide), wide)], traded[step - 1],
            tsend.at[step - 1], trecv.at[step - 1], tok - spot + to, feat,
        ))
        trades[-1].start()

    copies1, copies2 = {}, {}

    def project(k, step, low, high):
        return jnp.dot(
            lhs[k][step, :, low:high], rhs[k][low:high, :], preferred_element_type=jnp.float32
        )

    def to_mate(k, step):
        copies1[k, step] = remote(
            parts[k].at[step, pl.ds(pl.multiple_of((1 - core) * rows, rows), rows)],
            first[k].at[step], send1.at[k, step], recv1.at[k, step], tok, mate,
        )
        copies1[k, step].start()

    def onward(k, step):
        copies1[k, step].wait_recv()
        own = parts[k][step, pl.ds(pl.multiple_of(core * rows, rows), rows), :]
        held[k][step] = own + first[k][step]
        if step:
            copies2[k, step] = remote(
                held[k].at[step], second[k].at[step], send2.at[k, step], recv2.at[k, step],
                tok, ((pair + step) % chips) * 2 + core,
            )
            copies2[k, step].start()

    waiting = []
    for number, step in enumerate(order):
        for k in range(2):
            if number == 0:
                loads[k].wait()
            loads[k, step].wait()
            depth = lhs[k].shape[2]
            cut = depth // 2 if k else depth
            parts[k][step] = project(k, step, 0, cut)
            for item in waiting:
                onward(*item)
            waiting = []
            if cut < depth:
                parts[k][step] += project(k, step, cut, depth)
            to_mate(k, step)
            waiting = [(k, step)]
    for item in waiting:
        onward(*item)
    for k in range(2):
        total = held[k][0]
        for step in range(1, chips):
            copies2[k, step].wait_recv()
            total += second[k][step]
        outs[k][...] = total
    for copy in trades:
        copy.wait_recv()
    for copy in trades + list(copies1.values()) + list(copies2.values()):
        copy.wait_send()


def grads_kernel(sizes, part, slots, stored_rows, *refs):
    feats, group_toks, groups, local, rows, spacing, pieces, early = sizes
    total, out = refs[early : early + 2]
    recv, grads, heads, picked, scored, landed, late = refs[early + 2 : early + 9]
    sends, recvs, gsend, grecv, hsend, hrecv, psend, precv, ssend, srecv, lsend, lrecv = refs[
        early + 9 :
    ]
    highest = lax.Precision.HIGHEST
    near, count, height, rank = part.shape
    held = group_toks * local
    tall = height // pieces
    tok, feat = lax.axis_index("tok"), lax.axis_index("feat")
    group, spot = tok // group_toks, tok % group_toks
    me = spot * feats + feat

    def place(step):
        peer = (me + step) % count
        return peer // feats, peer % feats

    barrier = pltpu.get_barrier_semaphore()
    for step in range(1, count):
        peer_spot, peer_feat = place(step)
        greet(barrier, group * group_toks + peer_spot, peer_feat)

    @pl.when(group > 0)
    def _():
        greet(barrier, tok - group_toks, feat)

    @pl.when(group < groups - 1)
    def _():
        greet(barrier, tok + group_toks, feat)

    ends = (group > 0).astype(jnp.int32) + (group < groups - 1).astype(jnp.int32)
    pl.semaphore_wait(barrier, count - 1 + ends)

    copies = {}
    for piece in range(pieces):
        lines = pl.ds(piece * tall, tall)
        for step in range(1, count):
            peer_spot, peer_feat = place(step)
            copies[piece, step] = remote(
                part.at[:, peer_feat * group_toks + peer_spot, lines, :],
                recv.at[step, :, lines, :],
                sends.at[piece, step], recvs.at[piece, step],
                group * group_toks + peer_spot, peer_feat,
            )
            copies[piece, step].start()
    recv[0] = part[:, feat * group_toks + spot]
    width = late.shape[2]
    kept = pltpu.make_async_copy(
        stored_rows.at[:, pl.ds(pl.multiple_of(spot * width, width), width)], late.at[0], lsend.at[0]
    )
    kept.start()
    trades = []
    stored = [late.at[0], *refs[:early]] + [
        late.at[step - early] for step in range(early + 1, group_toks)
    ]

    terms = {}
    for source in range(count):
        base = (source // feats) * local + ((source % feats) * rows) // spacing
        for k in range(near):
            terms.setdefault(base + k, []).append((source, k))

    def block(at, piece):
        return grads.at[
            pl.ds(piece * tall, tall), pl.ds(pl.multiple_of(at * held, held), held), :
        ]

    def move(way, step, piece):
        at = jnp.clip(group - step if way == 0 else group + step, 0, groups - 1)
        to = tok + group_toks if way == 0 else tok - group_toks
        head = heads.at[at, pl.ds(piece * tall, tall), :]
        index = way, step, piece
        return (
            remote(block(at, piece), block(at, piece), gsend.at[index], grecv.at[index], to, feat),
            remote(head, head, hsend.at[index], hrecv.at[index], to, feat),
        )

    def each(way, step, piece, what, when):
        @pl.when(when)
        def _():
            for copy in move(way, step, piece):
                getattr(copy, what)()

    def sending(way, step):
        if way == 0:
            return (group - step >= 0) & (group + 1 < groups)
        return (group + step < groups) & (group - 1 >= 0)

    def taking(way, step):
        return group - 1 - step >= 0 if way == 0 else group + 1 + step < groups

    for piece in range(pieces):
        lines = pl.ds(piece * tall, tall)
        for step in range(1, count):
            copies[piece, step].wait_recv()
        for row in range(held + 1):
            value = None
            for source, k in terms.get(row, []):
                term = recv[(me + count - source) % count, k, lines, :]
                value = term if value is None else value + term
            if row == 0:
                heads[group, lines, :] = value
            else:
                block(group, piece)[:, row - 1, :] = value
        for way in range(2):
            if groups > 1:
                each(way, 0, piece, "start", sending(way, 0))
    for step in range(early + 1, group_toks):
        to = (spot + step) % group_toks
        trades.append(remote(
            stored_rows.at[:, pl.ds(pl.multiple_of(to * width, width), width)],
            late.at[step - early], lsend.at[step - early], lrecv.at[step - early],
            group * group_toks + to, feat,
        ))
        trades[-1].start()
    seqs = grads.shape[1]
    row = lax.broadcasted_iota(jnp.int32, (held, seqs), 0) + group * held
    pick = jnp.where(slots[...] == row, 1.0, 0.0).astype(jnp.float32)
    wide = height * rank
    part_wide = tall * rank
    first_lane = pl.multiple_of(spot * wide, wide)
    score = jnp.zeros((group_toks * late.shape[1], seqs), jnp.float32)

    def finish(piece, score):
        lines = range(piece * tall, (piece + 1) * tall)
        for at in range(1, groups):
            span = pl.ds(piece * tall, tall)
            grads[span, at * held - 1, :] += heads[at, span, :]
        for line in lines:
            lane = pl.ds(line * rank, rank)
            taken = jnp.dot(
                pick, grads[line], precision=highest, preferred_element_type=jnp.float32
            )
            for q in range(group_toks):
                picked[q, :, lane] = taken[q * local : (q + 1) * local]
        lanes = pl.ds(piece * part_wide, part_wide)
        mine = pl.ds(pl.multiple_of(first_lane + piece * part_wide, part_wide), part_wide)
        for step in range(1, group_toks):
            to = (spot + step) % group_toks
            trades.append(remote(
                picked.at[to, :, lanes], out.at[:, mine],
                psend.at[piece, step], precv.at[piece, step],
                group * group_toks + to, feat,
            ))
            trades[-1].start()
        out[:, mine] = picked[spot, :, lanes]
        if piece == 0:
            kept.wait()
            for copy in trades[: group_toks - 1 - early]:
                copy.wait_recv()
        for line in lines:
            lane = pl.ds(line * rank, rank)
            block_rows = jnp.concatenate([ref[:, lane] for ref in stored], axis=0)
            score += lax.dot_general(
                block_rows, grads[line], (((1,), (1,)), ((), ())),
                precision=highest, preferred_element_type=jnp.float32,
            )
        return score

    for step in range(max(groups - 1, 1)):
        for piece in range(pieces):
            if groups > 1:
                for way in range(2):
                    each(way, step, piece, "wait_recv", taking(way, step))
                    if step + 1 < groups - 1:
                        each(way, step + 1, piece, "start", sending(way, step + 1))
            if step >= groups - 2:
                for way in range(2):
                    for sent in range(groups - 1):
                        each(way, sent, piece, "wait_send", sending(way, sent))
                score = finish(piece, score)

    scored[...] = jnp.zeros_like(scored)
    few = scored.shape[2]
    for step in range(group_toks):
        for f in range(feats):
            first = (step * feats + f) * few
            scored[step, f, :, : score.shape[1]] = score[first : first + few]
    parts = []
    for step in range(group_toks):
        for turn in range(feats):
            if step or turn:
                to = (feat + turn) % feats
                parts.append(remote(
                    scored.at[step, to], landed.at[step, turn],
                    ssend.at[step, turn], srecv.at[step, turn],
                    group * group_toks + (spot + group_toks - step) % group_toks, to,
                ))
                parts[-1].start()
    summed = scored[0, feat]
    for number, copy in enumerate(parts, 1):
        copy.wait_recv()
        summed += landed[number // feats, number % feats]
    column = lax.broadcasted_iota(jnp.int32, (seqs, seqs), 0)
    by_slot = jnp.where(slots[...] == column, 1.0, 0.0).astype(jnp.float32)
    total[...] = lax.dot_general(
        summed[:, :seqs], by_slot, (((1,), (1,)), ((), ())),
        precision=highest, preferred_element_type=jnp.float32,
    )
    for copy in trades[group_toks - 1 - early :]:
        copy.wait_recv()
    for copy in trades + parts + list(copies.values()):
        copy.wait_send()


def body(
    activations,
    out_grads,
    proj_in,
    proj_out,
    left_factor,
    right_factor,
    seq_lengths,
    seq_slots,
    stored_grads,
):
    highest = lax.Precision.HIGHEST
    f32 = jnp.float32
    dma = pltpu.SemaphoreType.DMA
    feats, toks = lax.axis_size("feat"), lax.axis_size("tok")
    group_toks = 4 if toks % 4 == 0 else 1
    chips, groups, count = feats // 2, toks // group_toks, group_toks * feats
    rank = right_factor.shape[0]
    tok_rows = activations.shape[0]
    seq_count = seq_lengths.shape[0]
    local = seq_count // toks
    spacing = tok_rows // local
    rows = tok_rows // feats
    height = rank // count
    near = max(rows // spacing, 1) + 1
    feat, tok = lax.axis_index("feat"), lax.axis_index("tok")
    spot = tok % group_toks
    store_rows, width = stored_grads.shape
    wide = width // group_toks

    early = group_toks - 2
    any_space = pl.BlockSpec(memory_space=pl.ANY)
    lefts, mats = (out_grads, activations), (proj_out, proj_in)
    pair_rows = pltpu.VMEM((chips, rows, rank), f32)
    out_total, in_total, *traded = pl.pallas_call(
        functools.partial(project_kernel, (chips, rows, group_toks, early)),
        out_shape=[jax.ShapeDtypeStruct((rows, rank), f32)] * 2
        + [jax.ShapeDtypeStruct((store_rows, wide), f32)] * early,
        in_specs=[any_space] * 5,
        out_specs=[VMEM] * (2 + early),
        scratch_shapes=[pltpu.VMEM((chips, 2 * rows, m.shape[1]), m.dtype) for m in lefts]
        + [pltpu.VMEM(m.shape, m.dtype) for m in mats]
        + [pltpu.VMEM((chips, 2 * rows, rank), f32)] * 2
        + [pair_rows] * 6
        + [dma((2, chips + 1))]
        + [dma((2, chips))] * 4
        + [dma((early,))] * 2,
        compiler_params=pltpu.CompilerParams(
            collective_id=0, has_side_effects=True, vmem_limit_bytes=60 << 20
        ),
        name="project",
    )(*lefts, *mats, stored_grads)
    right_side = jnp.dot(in_total, right_factor, precision=highest)
    left_side = jnp.dot(out_total, left_factor.T, precision=highest)

    places = tok * tok_rows + feat * rows + jnp.arange(rows, dtype=jnp.int32)
    numbers = jnp.arange(seq_count, dtype=jnp.int32)
    close = tok * local + (feat * rows) // spacing - 1 + jnp.arange(near, dtype=jnp.int32)
    starts = jnp.sum(jnp.where(numbers[None, :] < close[:, None], seq_lengths[None, :], 0), axis=1)
    sizes = jnp.sum(jnp.where(numbers[None, :] == close[:, None], seq_lengths[None, :], 0), axis=1)
    inside = (places[:, None] >= starts[None, :]) & (places[:, None] < (starts + sizes)[None, :])
    weights = inside.astype(f32) / jnp.maximum(sizes, 1).astype(f32)[None, :]
    spread = jnp.concatenate([weights[:, k : k + 1] * left_side for k in range(near)], axis=1)
    part = lax.dot_general(spread, right_side, (((0,), (0,)), ((), ())), precision=highest)

    score_rows = store_rows // feats
    lanes = seq_count + -seq_count % 128
    pieces = 2 if height % 16 == 0 else 1
    hops = max(groups - 1, 1)
    sizes_ = (feats, group_toks, groups, local, rows, spacing, pieces, early)
    scores, own_rows = pl.pallas_call(
        functools.partial(grads_kernel, sizes_),
        out_shape=[
            jax.ShapeDtypeStruct((score_rows, seq_count), f32),
            jax.ShapeDtypeStruct((local, width), f32),
        ],
        in_specs=[VMEM] * 2 + [any_space] + [VMEM] * early,
        out_specs=[VMEM] * 2,
        scratch_shapes=[
            pltpu.VMEM((count, near, height, rank), f32),
            pltpu.VMEM((height, seq_count, rank), f32),
            pltpu.VMEM((groups, height, rank), f32),
            pltpu.VMEM((group_toks, local, wide), f32),
            pltpu.VMEM((group_toks, feats, score_rows, lanes), f32),
            pltpu.VMEM((group_toks, feats, score_rows, lanes), f32),
            pltpu.VMEM((group_toks - early, store_rows, wide), f32),
        ]
        + [dma((pieces, count))] * 2
        + [dma((2, hops, pieces))] * 4
        + [dma((pieces, group_toks))] * 2
        + [dma((group_toks, feats))] * 2
        + [dma((group_toks - early,))] * 2,
        compiler_params=pltpu.CompilerParams(collective_id=1, has_side_effects=True),
        name="grads",
    )(part.reshape(near, count, height, rank), seq_slots.reshape(1, seq_count), stored_grads, *traded)
    return scores, own_rows


def solution(mesh):
    placed = (
        P("tok", "feat"),
        P("tok", "feat"),
        P("feat", None),
        P("feat", None),
        P(),
        P(),
        P(),
        P(),
        P("tok", "feat"),
    )
    return jax.shard_map(
        body,
        mesh=mesh,
        in_specs=placed,
        out_specs=(P(("tok", "feat"), None), P("tok", "feat")),
        check_vma=False,
    )
```

profile of v0, /device:TPU:0, one launch (start us, length us, event | category | flops | bytes accessed | tf_op | source)
XLA Modules:
  0.0 86.3 jit_solution(8922665770513895169)
XLA Ops:
  0.6 0.0 copy-start
  0.7 0.9 %select_reduce_fusion.1 = (s32[3]{0:T(128)S(1)}, s32[3]{0:T(128)S(1)}) fusion(s32[64]{0:T(128)} %param.15, s32[3]{0:T(128)S(1)} %iota_add_fusion.1), kind=kLoop, calls=%fused_computation.12 | loop fusion | flops 1146 | bytes 292 | tf_op jit(solution)/shard_map/reduce_sum | solution.py:391
  1.6 0.1 convert_divide_fusion
  1.7 0.0 copy-start.1
  1.7 23.5 %project.1 = (f32[256,256]{1,0:T(8,128)}, f32[256,256]{1,0:T(8,128)}, f32[32,4096]{1,0:T(8,128)}, f32[32,4096]{1,0:T(8,128)}) custom-call(bf16[1024,2048]{1,0:T(8,128)(2,1)} %refs_0_.1, bf16[1024,7168]{1,0:T(8,128)(2,1)} %refs_1_.1, bf16[2048,256]{1,0:T(8,128)(2,1)} %refs_2_.1, bf16[7168,256]{1,0:T(8,128)(2,1)} %refs_3_.1, f32[32,16384]{1,0:T(8,128)} %stored_rows.1), custom_call_target="tpu_custom_call" | custom-call | tf_op jit(solution)/shard_map/project/pallas_call | solution.py:367
  25.2 0.0 copy-done.1
  25.2 1.3 %fusion.9 = f32[256,256]{1,0:T(8,128)S(1)} fusion(f32[256,256]{1,0:T(8,128)} %get-tuple-element.7, f32[256,256]{1,0:T(8,128)S(1)} %copy-done.1), kind=kOutput, calls=%fused_computation.20 | convolution fusion | flops 201326592 | bytes 786432 | tf_op jit(solution)/shard_map/dot_general | solution.py:385
  26.5 0.0 copy-done
  26.5 1.4 %broadcast_multiply_fusion.2 = (f32[256,256]{0,1:T(8,128)S(1)}, f32[256,256]{0,1:T(8,128)S(1)}, f32[256,256]{0,1:T(8,128)S(1)}) fusion(f32[256]{0:T(256)S(1)} %bitcast.11, f32[256]{0:T(256)S(1)} %bitcast.12, f32[256]{0:T(256)S(1)} %bitcast.13, f32[256,256]{1,0:T(8,128)} %get-tuple-element.6, f32[256,256]{1,0:T(8,128)S(1)} %copy-done), kind=kOutput, calls=%fused_computation.8 | convolution fusion | flops 201523200 | bytes 1313792 | tf_op jit(solution)/shard_map/dot_general | solution.py:386
  27.9 1.7 %fusion = f32[768,256]{1,0:T(8,128)} fusion(f32[256,256]{1,0:T(8,128)S(1)} %fusion.9, f32[256,256]{0,1:T(8,128)S(1)} %get-tuple-element.13, f32[256,256]{0,1:T(8,128)S(1)} %get-tuple-element.14, f32[256,256]{0,1:T(8,128)S(1)} %get-tuple-element.12), kind=kOutput, calls=%fused_computation | convolution fusion | flops 604372992 | bytes 1835008 | tf_op jit(solution)/shard_map/dot_general | solution.py:396
  29.6 53.6 %grads.1 = (f32[8,64]{1,0:T(8,128)}, f32[8,16384]{1,0:T(8,128)}) custom-call(f32[3,16,16,256]{3,2,1,0:T(8,128)} %bitcast.10, s32[1,64]{1,0:T(1,128)} %bitcast.14, f32[32,16384]{1,0:T(8,128)} %stored_rows.1, f32[32,4096]{1,0:T(8,128)} %get-tuple-element.8.refs_0_, f32[32,4096]{1,0:T(8,128)} %get-tuple-element.9.refs_1_), custom_call_target="tpu_custom_call" | custom-call | tf_op jit(solution)/shard_map/grads/pallas_call | solution.py:403
  83.2 1.3 %copy.13 = f32[8,64]{1,0:T(8,128)} copy(f32[8,64]{1,0:T(8,128)} %get-tuple-element.22) | data formatting | bytes 4096
  84.4 1.9 %copy.14 = f32[8,16384]{1,0:T(8,128)} copy(f32[8,16384]{1,0:T(8,128)} %get-tuple-element.23) | data formatting | bytes 1048576
  (4 shorter events, 0.0 us)
Async XLA Ops:
  0.6 25.9 %copy-start = (f32[256,256]{1,0:T(8,128)S(1)}, f32[256,256]{1,0:T(8,128)}, u32[]{:S(2)}) copy-start(f32[256,256]{1,0:T(8,128)} %param.13) | copy-start | bytes 786436
  1.7 23.5 %copy-start.1 = (f32[256,256]{1,0:T(8,128)S(1)}, f32[256,256]{1,0:T(8,128)}, u32[]{:S(2)}) copy-start(f32[256,256]{1,0:T(8,128)} %param.14) | copy-start | bytes 786436
where the time goes:
time: 87 us; the launch traced here: 86.3 us
  Pallas kernels  77.1 us (89%)
  matrix products  4.38 us (5%)
  local copies, waits for them, and re-layouts  3.14 us (4%)
  other arithmetic  0.99 us (1%)
    pallas_call x1, Pallas kernels, body(): pl.pallas_call(functools.partial(grads_kernel, sizes_), out_shape=[jax.Sh...  53.6 us
    pallas_call x1, Pallas kernels, body(): pl.pallas_call(functools.partial(project_kernel, (chips, rows, group_toks...  23.5 us
    unnamed x6, local copies, waits for them, and re-layouts  3.14 us

commit v1 on v0

v1 whole, which is shorter than its diff:
```python
import functools

import jax
import jax.numpy as jnp
from jax import lax
from jax.experimental import pallas as pl
from jax.experimental.pallas import tpu as pltpu
from jax.sharding import PartitionSpec as P

MESH = pl.DeviceIdType.MESH
VMEM = pl.BlockSpec(memory_space=pltpu.VMEM)
ANY = pl.BlockSpec(memory_space=pl.ANY)
F32, BF16 = jnp.float32, jnp.bfloat16
DOWN, UP = 0, 1


def halves(value):
    high = value.astype(BF16)
    return high, (value - high.astype(F32)).astype(BF16)


def times(left, right):
    return jnp.dot(left, right, preferred_element_type=F32)


def times_t(left, right):
    return lax.dot_general(left, right, (((1,), (1,)), ((), ())), preferred_element_type=F32)


def stack_left(value, axis):
    high, low = halves(value)
    return jnp.concatenate([high, low, high], axis=axis)


def stack_right(value, axis):
    high, low = halves(value)
    return jnp.concatenate([high, high, low], axis=axis)


def aligned(index, size):
    return pl.ds(pl.multiple_of(index * size, size), size)


def kernel(dims, *refs):
    toks, feats, local, chunk, rank, seqs, store_rows = dims
    out_rows, in_rows, out_mat, in_mat, left_hbm, right_hbm, lens_hbm, slots_hbm, stored = refs[:9]
    total, out = refs[9:11]
    lhs_o, lhs_i, rhs_o, rhs_i, left_f, right_f, lens, slots = refs[11:19]
    left_cat, right_cat = refs[19:21]
    lp, la, ly, lb, lfin = refs[21:26]
    rp, ra, ry, rb, rfull = refs[26:31]
    block, hx, hz, gs = refs[31:35]
    kept, given, mats, sc, picked, scored, landed = refs[35:42]
    load, asem, bsem, csem, xsem, hsem, zsend, zrecv, ssem, psem, rsem = refs[42:]

    tok, feat = lax.axis_index("tok"), lax.axis_index("feat")
    plane, x = tok // 2, tok % 2
    y, c = feat // 2, feat % 2
    planes = toks // 2
    mate, chips = feat + 1 - 2 * c, feats // 2
    across = [(y + turn) % chips for turn in range(1, chips)]
    beside = tok + 1 - 2 * x
    wide = rank // feats
    half_o = wide // 2
    quarters = half_o // 8
    in_plane = 2 * local
    half_lanes = half_o * rank
    part_lanes = 8 * rank
    tiles = rank // 128
    below, above = plane > 0, plane < planes - 1

    def remote(src, dst, sems, to_tok, to_feat):
        return pltpu.make_async_remote_copy(
            src_ref=src, dst_ref=dst, send_sem=sems[0], recv_sem=sems[1],
            device_id=(to_tok, to_feat), device_id_type=MESH,
        )

    small = [(left_hbm, left_f), (right_hbm, right_f), (lens_hbm, lens), (slots_hbm, slots)]
    loads = {}

    def fetch(key, src, dst):
        loads[key] = pltpu.make_async_copy(src, dst, load.at[len(loads)])
        loads[key].start()

    fetch("out", out_mat, rhs_o)
    fetch(("o", 0), out_rows.at[pl.ds(0, chunk)], lhs_o.at[0])
    fetch("left", *small[0])
    fetch("in", in_mat, rhs_i)
    fetch(("i", 0), in_rows.at[pl.ds(0, chunk)], lhs_i.at[0])
    for n, name in ((1, "right"), (2, "lens"), (3, "slots")):
        fetch(name, *small[n])
    for k in range(1, local):
        fetch(("o", k), out_rows.at[pl.ds(k * chunk, chunk)], lhs_o.at[k])
        fetch(("i", k), in_rows.at[pl.ds(k * chunk, chunk)], lhs_i.at[k])
    fetch("kept", stored.at[:, aligned(x, half_lanes)], kept)

    barrier = pltpu.get_barrier_semaphore()

    def greet(to_tok, to_feat):
        pl.semaphore_signal(barrier, inc=1, device_id=(to_tok, to_feat), device_id_type=MESH)

    for step in range(2):
        for turn in range(feats):
            if step or turn:
                greet(beside if step else tok, (feat + turn) % feats)
    neighbours = [
        (below, tok - 2), (above, tok + 2),
        (below & (x == 0), tok - 1), (above & (x == 1), tok + 1),
    ]
    met = 2 * feats - 1
    for there, other in neighbours:
        met += there.astype(jnp.int32)

        @pl.when(there)
        def _():
            greet(other, feat)

    sent = []

    def start(copy):
        copy.start()
        sent.append(copy)
        return copy

    pieces = given.shape[1] // (2 * rank)
    trades = []

    def trade(count):
        for _ in range(count):
            n = len(trades)
            if n < pieces:
                lanes = pl.ds(n * 2 * rank, 2 * rank)
                first = pl.multiple_of((1 - x) * half_lanes + n * 2 * rank, 2 * rank)
                trades.append(start(remote(
                    stored.at[:, pl.ds(first, 2 * rank)], given.at[:, lanes],
                    (ssem.at[0, n], ssem.at[1, n]), beside, feat,
                )))

    copies = {}

    def project_out(k):
        loads["o", k].wait()
        if k == 0:
            loads["out"].wait()
        sums = times(lhs_o[k], rhs_o[...])
        if k == 0:
            loads["left"].wait()
            for core in range(2):
                for side in range(chips):
                    rows = left_f[pl.ds((side * 2 + core) * wide, wide), :]
                    left_cat[pl.ds((core * chips + side) * wide, wide), :] = stack_left(rows, 1)
        lp[k] = times_t(left_cat[...], stack_right(sums, 1)).reshape(2, chips, wide, chunk)
        if k == 0:
            pl.semaphore_wait(barrier, met)
            trade(3)
        copies["a", 0, k] = start(remote(
            lp.at[k, 1 - c], la.at[k], (asem.at[0, 0, k], asem.at[1, 0, k]), tok, mate))

    def pair_left(k):
        copies["a", 0, k].wait_recv()
        ly[k] = lp[k, c] + la[k]
        for n, other in enumerate(across):
            copies["b", 0, k, n] = start(remote(
                ly.at[k, other], lb.at[k, n], (bsem.at[0, 0, k, n], bsem.at[1, 0, k, n]),
                tok, other * 2 + c))

    def project_in(k):
        if k == 0:
            loads["in"].wait()
        loads["i", k].wait()
        depth = lhs_i.shape[2]
        cut = depth // 2
        sums = times(lhs_i[k, :, :cut], rhs_i[:cut, :])
        rp[k] = sums.reshape(2, chunk // 2, rank)
        pair_left(k)
        sums = times(lhs_i[k, :, cut:], rhs_i[cut:, :])
        rp[k] += sums.reshape(2, chunk // 2, rank)
        copies["a", 1, k] = start(remote(
            rp.at[k, 1 - c], ra.at[k], (asem.at[0, 1, k], asem.at[1, 1, k]), tok, mate))

    def pair_right(k):
        copies["a", 1, k].wait_recv()
        ry[k] = rp[k, c] + ra[k]
        for n, other in enumerate(across):
            copies["b", 1, k, n] = start(remote(
                ry.at[k], rb.at[k, n], (bsem.at[0, 1, k, n], bsem.at[1, 1, k, n]),
                tok, other * 2 + c))

    def finish_rows(k):
        if k == 0:
            loads["right"].wait()
            right_cat[...] = stack_right(right_f[...], 0)
        left, rows = ly[k, y], ry[k]
        for n in range(chips - 1):
            copies["b", 0, k, n].wait_recv()
            left += lb[k, n]
        lfin[k] = left
        for n in range(chips - 1):
            copies["b", 1, k, n].wait_recv()
            rows += rb[k, n]
        rfull[k, c] = times(stack_left(rows, 1), right_cat[...])
        copies["c", k] = start(remote(
            rfull.at[k, c], rfull.at[k, c], (csem.at[0, k], csem.at[1, k]), tok, mate))

    spans = {}

    def starts_of():
        loads["lens"].wait()
        lengths = lens[...].astype(F32)
        number = lax.broadcasted_iota(jnp.int32, (local, seqs), 1)
        mine = lax.broadcasted_iota(jnp.int32, (local, seqs), 0) + tok * local

        def pick(mask):
            return jnp.sum(jnp.where(mask, lengths, 0.0), axis=1, keepdims=True)

        spans["start"] = pick(number < mine)
        spans["now"] = 1.0 / jnp.maximum(pick(number == mine), 1.0)
        spans["before"] = 1.0 / jnp.maximum(pick(number == mine - 1), 1.0)

    def seq_rows(at_plane, number, side, count=1):
        first = (at_plane * in_plane + number * 2 + side) * 8
        return pl.ds(pl.multiple_of(first, 8), 8 * count)

    def settle(k, value):
        for tile in range(tiles):
            part = value[:, tile * 128 : (tile + 1) * 128]
            block[k, :, :, tile] = part.reshape(2, quarters, 8, 128)
        if k < local:
            gs[:, :, seq_rows(plane, k, x), :] = block[k, x]
            copies["x", k] = start(remote(
                block.at[k, 1 - x], gs.at[:, :, seq_rows(plane, k, x), :],
                (xsem.at[0, k], xsem.at[1, k]), beside, feat))

    def head_copies():
        return (
            (x == 1, remote(block.at[local, 0], hx, (hsem.at[0, 0], hsem.at[1, 0]), beside, feat)),
            ((x == 0) & below, remote(
                block.at[local, 0], hz, (hsem.at[0, 1], hsem.at[1, 1]), tok - 2, feat)),
            ((x == 0) & below, remote(
                block.at[local, 1], hz, (hsem.at[0, 2], hsem.at[1, 1]), tok - 1, feat)),
        )

    carry = {}

    def gradients(k):
        if k == 0:
            starts_of()
        copies["c", k].wait_recv()
        places = lax.broadcasted_iota(jnp.int32, (1, chunk), 1) + (tok * local + k) * chunk
        inside = places.astype(F32) >= spans["start"][k : k + 1]
        now = jnp.where(inside, spans["now"][k : k + 1], 0.0)
        before = jnp.where(inside, 0.0, spans["before"][k : k + 1])
        left = lfin[k]
        weighted = jnp.concatenate([left * now, left * before], axis=0)
        right = rfull[k].reshape(chunk, rank)
        both = times(stack_left(weighted, 1), stack_right(right, 0))
        tail = both[wide:]
        if k:
            settle(k - 1, carry["sum"] + tail)
        else:
            settle(local, tail)
            for when, copy in head_copies():
                pl.when(when)(copy.start)
        carry["sum"] = both[:wide]
        if k == local - 1:
            settle(k, carry["sum"])

    ways = (DOWN, UP)

    def block_plane(way, step):
        return jnp.clip(plane + step if way == DOWN else plane - step, 0, planes - 1)

    def sending(way, step):
        if way == DOWN:
            return below & (plane + step < planes)
        return above & (plane - step >= 0)

    def taking(way, step):
        return plane + 1 + step < planes if way == DOWN else plane - 1 - step >= 0

    def parts_of(step):
        return local if step == 0 else local // 2 if step == 1 else quarters

    def z_copy(way, step, part):
        at = block_plane(way, step)
        if step < 2:
            count = 1 if step == 0 else 2
            piece = gs.at[:, :, seq_rows(at, part * count, 0, 2 * count), :]
        else:
            piece = gs.at[part, :, seq_rows(at, 0, 0, in_plane), :]
        return remote(
            piece, piece, (zsend.at[way, step, part], zrecv.at[way, step, part]),
            tok - 2 if way == DOWN else tok + 2, feat,
        )

    def z_each(way, step, part, what, when):
        @pl.when(when)
        def _():
            getattr(z_copy(way, step, part), what)()

    last_step = max(planes - 2, 0)

    def complete(k):
        copies["x", k].wait_recv()
        if k == local - 1:
            @pl.when(x == 1)
            def _():
                gs[:, :, seq_rows(plane, k, 0), :] += block[local, 1]

            @pl.when(x == 0)
            def _():
                head_copies()[0][1].wait_recv()
                gs[:, :, seq_rows(plane, k, 0), :] += hx[...]

            @pl.when(above)
            def _():
                head_copies()[1][1].wait_recv()
                gs[:, :, seq_rows(plane, k, 1), :] += hz[...]
        if planes > 1:
            for way in ways:
                z_each(way, 0, k, "start", sending(way, 0))

    def take(step, parts, onward):
        if step > last_step or planes < 2:
            return
        for part in parts:
            for way in ways:
                z_each(way, step, part, "wait_recv", taking(way, step))
        if step < last_step:
            for part in onward:
                for way in ways:
                    z_each(way, step + 1, part, "start", sending(way, step + 1))

    def make_mats(rows, lanes, value):
        high, low = halves(value)
        count = 2 * store_rows
        mats[pl.ds(rows * store_rows, store_rows), lanes] = high
        mats[pl.ds(count + rows * store_rows, store_rows), lanes] = low

    def score(at, part):
        lines = []
        for line in range(8):
            first = at * in_plane * 8 + line
            for tile in range(tiles):
                lines.append(gs[part, tile, pl.ds(first, in_plane, stride=8), :])
        high, low = halves(jnp.concatenate(lines, axis=1))
        return times_t(
            jnp.concatenate([high, low], axis=0),
            mats[:, pl.ds(part * part_lanes, part_lanes)],
        )

    def score_plane(at):
        value = score(at, 0)
        for part in range(1, quarters):
            value += score(at, part)
        sc[at] = value

    def score_step(step):
        for way in ways:
            @pl.when(taking(way, step))
            def _():
                score_plane(block_plane(way, step + 1))

    def stage_rows(k):
        if 0 <= k < local:
            finish_rows(k)

    def stage_grads(k):
        if 0 <= k < local:
            gradients(k)
            trade(1)

    def stage_complete(k):
        if 0 <= k < local:
            complete(k)
            group = k // 2 - 1
            if k % 2 == 0 and group >= 0:
                take(0, (2 * group, 2 * group + 1), (group,))

    rows_done, grads_done = 0, 0
    for k in range(local):
        project_out(k)
        if k:
            pair_right(k - 1)
        project_in(k)
        if 0 < k < 4:
            trade(1)
        if k >= 2 and k % 2 == 0:
            stage_rows(rows_done)
            rows_done += 1
        elif k >= 3:
            stage_grads(grads_done)
            grads_done += 1
            stage_complete(grads_done - 3)
    pair_right(local - 1)
    while grads_done < local:
        if rows_done == grads_done:
            stage_rows(rows_done)
            rows_done += 1
        stage_complete(grads_done - 2)
        stage_grads(grads_done)
        grads_done += 1
    trade(pieces)
    stage_complete(local - 2)
    loads["kept"].wait()
    make_mats(0, pl.ds(0, half_lanes), kept[...])
    stage_complete(local - 1)

    loads["slots"].wait()
    at_row = lax.broadcasted_iota(jnp.int32, (seqs, seqs), 1)
    seq_of = ((at_row // in_plane) * 2 + at_row % 2) * local + (at_row % in_plane) // 2
    order = jnp.where(lax.broadcasted_iota(jnp.int32, (seqs, seqs), 0) == seq_of, 1.0, 0.0)
    slot = lax.broadcasted_iota(jnp.int32, (seqs, seqs), 0)
    by_slot = times(
        jnp.where(slots[...] == slot, 1.0, 0.0).astype(BF16), order.astype(BF16))
    row = lax.broadcasted_iota(jnp.int32, (2 * local, seqs), 0)
    wanted = jnp.where(row < local, tok * local + row, beside * local + row - local)
    pick = times(
        jnp.where(slots[...] == wanted, 1.0, 0.0).astype(BF16), order.astype(BF16)).astype(BF16)
    pick = jnp.concatenate([pick, pick], axis=1)

    groups = local // 2
    for copy in trades:
        copy.wait_recv()
    make_mats(1, pl.ds(0, half_lanes), given[...])
    take(0, (local - 2, local - 1), (groups - 1,))
    score_plane(plane)
    if last_step > 0:
        score_step(0)
        take(1, range(groups), range(quarters))
        if last_step > 1:
            score_step(1)
        for step in range(2, last_step):
            take(step, range(quarters), range(quarters))
            score_step(step)

    def rows_for_slots(part):
        for line in range(8):
            high, low = halves(jnp.concatenate(
                [gs[part, tile, pl.ds(line, seqs, stride=8), :] for tile in range(tiles)], axis=1))
            taken = times(pick, jnp.concatenate([high, low], axis=0))
            lane = part * part_lanes + line * rank
            out[:, pl.ds(pl.multiple_of(x * half_lanes + lane, rank), rank)] = taken[:local]
            picked[:, pl.ds(lane, rank)] = taken[local:]
        there = pl.ds(pl.multiple_of(x * half_lanes + part * part_lanes, part_lanes), part_lanes)
        copies["p", part] = start(remote(
            picked.at[:, pl.ds(part * part_lanes, part_lanes)], out.at[:, there],
            (psem.at[0, part], psem.at[1, part]), beside, feat))

    by_part = last_step >= 2
    for part in range(quarters):
        if by_part:
            take(last_step, (part,), ())
        rows_for_slots(part)
    if planes > 1:
        score_step(last_step)

    count = 2 * store_rows
    sums = sc[...]
    high_high, high_low, low_high = sums[:, :in_plane], sums[:, :in_plane], sums[:, in_plane:]
    by_row = (
        high_high[:, :, :count] + high_low[:, :, count:] + low_high[:, :, :count]
    ).reshape(seqs, count)
    few = scored.shape[2]
    lanes = scored.shape[3]
    placed = jnp.dot(by_slot, by_row, precision=lax.Precision.HIGHEST, preferred_element_type=F32)
    square = jnp.zeros((lanes, 128 - count), F32)
    tall = jnp.zeros((lanes - seqs, count), F32)
    if lanes > seqs:
        placed = jnp.concatenate([placed, tall], axis=0)
    turned = jnp.transpose(jnp.concatenate([placed, square], axis=1))
    for step in range(2):
        for f in range(feats):
            first = (step * feats + f) * few
            scored[step, f] = turned[first : first + few]
    parts = []
    for step in range(2):
        for turn in range(feats):
            if step or turn:
                to = (feat + turn) % feats
                parts.append(start(remote(
                    scored.at[step, to], landed.at[step, turn],
                    (rsem.at[0, step, turn], rsem.at[1, step, turn]),
                    beside if step else tok, to,
                )))
    summed = scored[0, feat]
    for number, copy in enumerate(parts, 1):
        copy.wait_recv()
        summed += landed[number // feats, number % feats]
    total[...] = summed[:, :seqs]

    for part in range(quarters):
        copies["p", part].wait_recv()
    for copy in sent:
        copy.wait_send()
    for when, copy in head_copies():
        pl.when(when)(copy.wait_send)
    if planes > 1:
        for step in range(last_step + 1):
            for way in ways:
                for part in range(parts_of(step)):
                    z_each(way, step, part, "wait_send", sending(way, step))


def body(
    activations,
    out_grads,
    proj_in,
    proj_out,
    left_factor,
    right_factor,
    seq_lengths,
    seq_slots,
    stored_grads,
):
    dma = pltpu.SemaphoreType.DMA
    feats, toks = lax.axis_size("feat"), lax.axis_size("tok")
    rank = right_factor.shape[0]
    tok_rows = activations.shape[0]
    seqs = seq_lengths.shape[0]
    local = seqs // toks
    chunk = tok_rows // local
    store_rows, width = stored_grads.shape
    planes, chips = toks // 2, feats // 2
    wide = rank // feats
    quarters = wide // 16
    tiles = rank // 128
    score_rows = store_rows // feats
    lanes = seqs + -seqs % 128
    half = chunk // 2
    steps = max(planes - 1, 1)
    pieces = width // 2 // (2 * rank)

    def vmem(*shape, dtype=F32):
        return pltpu.VMEM(shape, dtype)

    scores, own_rows = pl.pallas_call(
        functools.partial(kernel, (toks, feats, local, chunk, rank, seqs, store_rows)),
        out_shape=[
            jax.ShapeDtypeStruct((score_rows, seqs), F32),
            jax.ShapeDtypeStruct((local, width), F32),
        ],
        in_specs=[ANY] * 9,
        out_specs=[VMEM] * 2,
        scratch_shapes=[
            vmem(local, chunk, out_grads.shape[1], dtype=BF16),
            vmem(local, chunk, activations.shape[1], dtype=BF16),
            vmem(*proj_out.shape, dtype=BF16),
            vmem(*proj_in.shape, dtype=BF16),
            vmem(rank, rank),
            vmem(rank, rank),
            vmem(1, seqs, dtype=jnp.int32),
            vmem(1, seqs, dtype=jnp.int32),
            vmem(rank, 3 * rank, dtype=BF16),
            vmem(3 * rank, rank, dtype=BF16),
            vmem(local, 2, chips, wide, chunk),
            vmem(local, chips, wide, chunk),
            vmem(local, chips, wide, chunk),
            vmem(local, chips - 1, wide, chunk),
            vmem(local, wide, chunk),
            vmem(local, 2, half, rank),
            vmem(local, half, rank),
            vmem(local, half, rank),
            vmem(local, chips - 1, half, rank),
            vmem(local, 2, half, rank),
            vmem(local + 1, 2, quarters, tiles, 8, 128),
            vmem(quarters, tiles, 8, 128),
            vmem(quarters, tiles, 8, 128),
            vmem(quarters, tiles, seqs * 8, 128),
            vmem(store_rows, width // 2),
            vmem(store_rows, width // 2),
            vmem(4 * store_rows, width // 2, dtype=BF16),
            vmem(planes, 4 * local, 4 * store_rows),
            vmem(local, width // 2),
            vmem(2, feats, score_rows, lanes),
            vmem(2, feats, score_rows, lanes),
            dma((2 * local + 7,)),
            dma((2, 2, local)),
            dma((2, 2, local, chips - 1)),
            dma((2, local)),
            dma((2, local)),
            dma((2, 3)),
            dma((2, steps, local)),
            dma((2, steps, local)),
            dma((2, pieces)),
            dma((2, quarters)),
            dma((2, 2, feats)),
        ],
        compiler_params=pltpu.CompilerParams(
            collective_id=0, has_side_effects=True, vmem_limit_bytes=60 << 20
        ),
        name="influence",
    )(
        out_grads, activations, proj_out, proj_in, left_factor, right_factor,
        seq_lengths.reshape(1, seqs), seq_slots.reshape(1, seqs), stored_grads,
    )
    return scores, own_rows


def solution(mesh):
    placed = (
        P("tok", "feat"),
        P("tok", "feat"),
        P("feat", None),
        P("feat", None),
        P(),
        P(),
        P(),
        P(),
        P("tok", "feat"),
    )
    return jax.shard_map(
        body,
        mesh=mesh,
        in_specs=placed,
        out_specs=(P(("tok", "feat"), None), P("tok", "feat")),
        check_vma=False,
    )
```

time: 87 us -> 79.1 us (0.909)
  matrix products: 4.38 us -> 0 us
  Pallas kernels: 77.1 us -> 75.2 us
  other arithmetic: 0.99 us -> 0 us
    dot_general x3 -> x0, matrix products: 4.38 us -> none  [the longest x1 1.68 us: body(): lax.dot_general(spread, right_side, (((0,), (0,)), ((), ())), precision=h...]
    pallas_call x2 -> x1, Pallas kernels: 77.1 us -> 75.2 us  [body(): pl.pallas_call(functools.partial(kernel, (toks, feats, local, chunk, rank...]
    reduce_sum x1 -> x0, other arithmetic: 0.9 us -> none  [body(): jnp.sum(jnp.where(numbers[None, :] < close[:, None], seq_lengths[None, :]...]
    unnamed x6 -> x2, local copies, waits for them, and re-layouts: 3.14 us -> 3.13 us
where the time goes in v1:
time: 79.1 us; the launch traced here: 78.9 us
  Pallas kernels  75.2 us (95%)
  local copies, waits for them, and re-layouts  3.13 us (4%)
    pallas_call x1, Pallas kernels, body(): pl.pallas_call(functools.partial(kernel, (toks, feats, local, chunk, rank...  75.2 us
    unnamed x2, local copies, waits for them, and re-layouts  3.13 us

profile of v1, /device:TPU:0, one launch (start us, length us, event | category | flops | bytes accessed | tf_op | source)
XLA Modules:
  0.0 78.9 jit_solution(15780763910764299474)
XLA Ops:
  0.6 75.2 %influence.1 = (f32[8,64]{1,0:T(8,128)}, f32[8,16384]{1,0:T(8,128)}) custom-call(bf16[1024,2048]{1,0:T(8,128)(2,1)} %refs_0_.1, bf16[1024,7168]{1,0:T(8,128)(2,1)} %refs_1_.1, bf16[2048,256]{1,0:T(8,128)(2,1)} %refs_2_.1, bf16[7168,256]{1,0:T(8,128)(2,1)} %refs_3_.1, f32[256,256]{1,0:T(8,128)} %refs_4_.1, f32[256,256]{1,0:T(8,128)} %refs_5_.1, ...), custom_call_target="tpu_custom_call" | custom-call | tf_op jit(solution)/shard_map/influence/pallas_call | solution.py:537
  75.8 1.3 %copy.13 = f32[8,64]{1,0:T(8,128)} copy(f32[8,64]{1,0:T(8,128)} %get-tuple-element.4) | data formatting | bytes 4096
  77.1 1.9 %copy.14 = f32[8,16384]{1,0:T(8,128)} copy(f32[8,16384]{1,0:T(8,128)} %get-tuple-element.5) | data formatting | bytes 1048576

commit v2 on v1

v2 whole, which is shorter than its diff:
```python
import functools

import jax
import jax.numpy as jnp
from jax import lax
from jax.experimental import pallas as pl
from jax.experimental.pallas import tpu as pltpu
from jax.sharding import PartitionSpec as P

MESH = pl.DeviceIdType.MESH
VMEM = pl.BlockSpec(memory_space=pltpu.VMEM)
ANY = pl.BlockSpec(memory_space=pl.ANY)
F32, BF16 = jnp.float32, jnp.bfloat16
DOWN, UP = 0, 1


def halves(value):
    high = value.astype(BF16)
    return high, (value - high.astype(F32)).astype(BF16)


def times(left, right):
    return jnp.dot(left, right, preferred_element_type=F32)


def times_t(left, right):
    return lax.dot_general(left, right, (((1,), (1,)), ((), ())), preferred_element_type=F32)


def stack_left(value, axis):
    high, low = halves(value)
    return jnp.concatenate([high, low, high], axis=axis)


def stack_right(value, axis):
    high, low = halves(value)
    return jnp.concatenate([high, high, low], axis=axis)


def aligned(index, size):
    return pl.ds(pl.multiple_of(index * size, size), size)


def pushed_quarters(planes, quarters):
    return quarters // 4 if planes == 4 else 0


def both(first, second):
    if first is True:
        return second
    if second is True:
        return first
    return False if first is False or second is False else first & second


def no(value):
    return not value if isinstance(value, bool) else jnp.logical_not(value)


def when(condition, action):
    if condition is True:
        action()
    elif condition is not False:
        pl.when(condition)(action)


def kernel(dims, *refs):
    toks, feats, local, chunk, rank, seqs, store_rows = dims
    out_rows, in_rows, out_mat, in_mat, left_hbm, right_hbm, lens_hbm, slots_hbm, stored = refs[:9]
    total, out = refs[9:11]
    lhs_o, lhs_i, rhs_o, rhs_i, left_f, right_f, lens, slots = refs[11:19]
    left_cat, right_cat, folded = refs[19:22]
    lp, la, ly, lb, lfin = refs[22:27]
    rp, ra, ry, rb, rfull = refs[27:32]
    block, hx, hz, gs = refs[32:36]
    kept, given, guest, mats, guest_mats, sc, guest_sc = refs[36:43]
    found, picked, scored, landed = refs[43:47]
    load, asem, bsem, csem, xsem, hsem, zrecv, zrecv_late, srecv, precv, rrecv = refs[47:58]
    asent, bsent, csent, xsent, hsent, zsent, ssent, psent, rsent, wsent = refs[58:]

    tok, feat = lax.axis_index("tok"), lax.axis_index("feat")
    plane, x = tok // 2, tok % 2
    y, c = feat // 2, feat % 2
    planes = toks // 2
    mate, chips = feat + 1 - 2 * c, feats // 2
    across = [(y + turn) % chips for turn in range(1, chips)]
    beside = tok + 1 - 2 * x
    wide = rank // feats
    half_o = wide // 2
    quarters = half_o // 8
    in_plane = 2 * local
    half_lanes = half_o * rank
    part_lanes = 8 * rank
    tiles = rank // 128
    below, above = plane > 0, plane < planes - 1
    pushed = pushed_quarters(planes, quarters)
    outer = inner = False
    if pushed:
        outer = (plane == 0) | (plane == planes - 1)
        inner = (plane == 1) | (plane == planes - 2)
    partner = jnp.where(plane == 0, 1, jnp.where(
        plane == planes - 1, planes - 2, jnp.where(plane == 1, 0, planes - 1)))

    def remote(src, dst, sems, to_tok, to_feat):
        return pltpu.make_async_remote_copy(
            src_ref=src, dst_ref=dst, send_sem=sems[0], recv_sem=sems[1],
            device_id=(to_tok, to_feat), device_id_type=MESH,
        )

    loads = {}
    span = 2 if local % 2 == 0 else 1
    blocks = local // span
    tall = span * chunk

    def fetch(key, src, dst):
        loads[key] = pltpu.make_async_copy(src, dst, load.at[len(loads)])
        loads[key].start()

    def fetch_block(b):
        if b < blocks:
            rows = pl.ds(b * tall, tall)
            fetch(("i", b), in_rows.at[rows], lhs_i.at[rows])
            fetch(("o", b), out_rows.at[rows], lhs_o.at[rows])

    fetch("left", left_hbm, left_f)
    fetch("out", out_mat, rhs_o)
    fetch("in", in_mat, rhs_i)
    fetch_block(0)
    fetch("lens", lens_hbm, lens)
    fetch("slots", slots_hbm, slots)
    fetch("right", right_hbm, right_f)

    barrier = pltpu.get_barrier_semaphore()

    def greet(to_tok, to_feat):
        pl.semaphore_signal(barrier, inc=1, device_id=(to_tok, to_feat), device_id_type=MESH)

    for step in range(2):
        for turn in range(feats):
            if step or turn:
                greet(beside if step else tok, (feat + turn) % feats)
    met = 2 * feats - 1
    for side, there, crossing in ((-1, below, 0), (1, above, 1)):
        near = False
        if pushed:
            near = (outer & (partner == plane + side)) | (inner & (partner == plane + side))
        plain = both(there, no(near))
        corner = both(plain, x == crossing)
        met += plain.astype(jnp.int32) + corner.astype(jnp.int32)

        def greet_all(side=side):
            for other in range(2):
                for f in range(feats):
                    greet((plane + side) * 2 + other, f)

        if pushed:
            met += 2 * feats * near.astype(jnp.int32)
        when(near, greet_all)
        when(plain, lambda side=side: greet(tok + 2 * side, feat))
        when(corner, lambda side=side: greet(tok + side, feat))

    sent = []

    def start(copy, condition=True):
        when(condition, copy.start)
        return copy

    def await_sent(src, sem, condition=True):
        copy = remote(src, src, (sem, sem), tok, mate)
        sent.append((condition, copy))

    def await_all(dst, sem, condition=True):
        copy = remote(dst, dst, (sem, sem), tok, mate)
        when(condition, copy.wait_recv)

    piece = 2 * rank
    pieces = half_lanes // piece
    aside = pushed * part_lanes // piece
    trades = []

    def column(half, first, count=1):
        lanes = half * half_lanes + first * piece
        return pl.ds(pl.multiple_of(lanes, piece), piece * count)

    def push_own():
        copy = remote(
            stored.at[:, column(x, 0, aside)], guest.at[0], (ssent.at[2], srecv.at[2]),
            partner * 2 + x, feat)
        start(copy, outer)
        await_sent(stored.at[:, column(x, 0, aside)], ssent.at[2], outer)

    def push_given():
        lanes = pl.ds(0, aside * piece)
        await_all(given.at[:, lanes], srecv.at[0], outer)
        copy = remote(
            given.at[:, lanes], guest.at[1], (ssent.at[3], srecv.at[3]), partner * 2 + x, feat)
        start(copy, outer)
        await_sent(given.at[:, lanes], ssent.at[3], outer)

    def trade(count):
        for _ in range(count):
            n = len(trades)
            if n < pieces:
                kind = 0 if n < aside else 1
                trades.append(start(remote(
                    stored.at[:, column(1 - x, n)], given.at[:, pl.ds(n * piece, piece)],
                    (ssent.at[kind], srecv.at[kind]), beside, feat,
                )))

    def trades_sent():
        if aside:
            await_sent(stored.at[:, column(1 - x, 0, aside)], ssent.at[0])
        await_sent(stored.at[:, column(1 - x, aside, pieces - aside)], ssent.at[1])

    copies = {}

    def fold_left():
        loads["left"].wait()
        for core in range(2):
            for side in range(chips):
                rows = left_f[pl.ds((side * 2 + core) * wide, wide), :]
                high, low = halves(rows)
                left_cat[0, pl.ds((core * chips + side) * wide, wide), :] = high
                left_cat[1, pl.ds((core * chips + side) * wide, wide), :] = low
        loads["out"].wait()
        depth = rhs_o.shape[0]
        step = min(256, depth)
        for n in range(depth // step):
            rows = rhs_o[pl.ds(n * step, step), :]
            folded[0, pl.ds(n * step, step), :], folded[1, pl.ds(n * step, step), :] = halves(
                times_t(rows, left_cat[0]) + times_t(rows, left_cat[1]))

    def project_out(b):
        loads["o", b].wait()
        own = [lhs_o[pl.ds((b * span + n) * chunk, chunk), :] for n in range(span)]
        sums = [times(rows, folded[0]) + times(rows, folded[1]) for rows in own]
        for n in range(span):
            lp[b * span + n] = jnp.transpose(sums[n]).reshape(2, chips, wide, chunk)

    def send_left(b):
        for k in range(b * span, b * span + span):
            copies["a", 0, k] = start(remote(
                lp.at[k, 1 - c], la.at[k], (asent.at[0], asem.at[0, k]), tok, mate))

    def pair_left(k):
        copies["a", 0, k].wait_recv()
        ly[k] = lp[k, c] + la[k]
        for n, other in enumerate(across):
            copies["b", 0, k, n] = start(remote(
                ly.at[k, other], lb.at[k, n], (bsent.at[0, n], bsem.at[0, k, n]),
                tok, other * 2 + c))

    def project_in(b):
        if b == 0:
            loads["in"].wait()
        loads["i", b].wait()
        fetch_block(b + 2)
        own = [lhs_i[pl.ds((b * span + n) * chunk, chunk), :] for n in range(span)]
        for n, sums in enumerate([times(rows, rhs_i[...]) for rows in own]):
            rp[b * span + n] = sums.reshape(2, chunk // 2, rank)

    def send_right(b):
        for k in range(b * span, b * span + span):
            copies["a", 1, k] = start(remote(
                rp.at[k, 1 - c], ra.at[k], (asent.at[1], asem.at[1, k]), tok, mate))

    def pair_right(k):
        copies["a", 1, k].wait_recv()
        ry[k] = rp[k, c] + ra[k]
        for n, other in enumerate(across):
            copies["b", 1, k, n] = start(remote(
                ry.at[k], rb.at[k, n], (bsent.at[1, n], bsem.at[1, k, n]),
                tok, other * 2 + c))

    def rows_sent():
        for side, ref in ((0, lp), (1, rp)):
            await_sent(ref.at[:, 1 - c], asent.at[side])
        for n, other in enumerate(across):
            await_sent(ly.at[:, other], bsent.at[0, n])
            await_sent(ry, bsent.at[1, n])
        await_sent(rfull.at[:, c], csent.at[0])
        await_sent(block.at[pl.ds(0, local), 1 - x], xsent.at[0])

    def finish_rows(k):
        if k == 0:
            loads["right"].wait()
            right_cat[...] = stack_right(right_f[...], 0)
        left, rows = ly[k, y], ry[k]
        for n in range(chips - 1):
            copies["b", 0, k, n].wait_recv()
            left += lb[k, n]
        lfin[k] = left
        for n in range(chips - 1):
            copies["b", 1, k, n].wait_recv()
            rows += rb[k, n]
        rfull[k, c] = times(stack_left(rows, 1), right_cat[...])
        copies["c", k] = start(remote(
            rfull.at[k, c], rfull.at[k, c], (csent.at[0], csem.at[k]), tok, mate))

    spans = {}

    def starts_of():
        loads["lens"].wait()
        lengths = lens[...].astype(F32)
        number = lax.broadcasted_iota(jnp.int32, (local, seqs), 1)
        mine = lax.broadcasted_iota(jnp.int32, (local, seqs), 0) + tok * local

        def pick(mask):
            return jnp.sum(jnp.where(mask, lengths, 0.0), axis=1, keepdims=True)

        spans["start"] = pick(number < mine)
        spans["now"] = 1.0 / jnp.maximum(pick(number == mine), 1.0)
        spans["before"] = 1.0 / jnp.maximum(pick(number == mine - 1), 1.0)

    def seq_rows(at_plane, number, side, count=1):
        first = (at_plane * in_plane + number * 2 + side) * 8
        return pl.ds(pl.multiple_of(first, 8), 8 * count)

    def settle(k, value):
        for tile in range(tiles):
            part = value[:, tile * 128 : (tile + 1) * 128]
            block[k, :, :, tile] = part.reshape(2, quarters, 8, 128)
        if k < local:
            gs[:, :, seq_rows(plane, k, x), :] = block[k, x]
            copies["x", k] = start(remote(
                block.at[k, 1 - x], gs.at[:, :, seq_rows(plane, k, x), :],
                (xsent.at[0], xsem.at[k]), beside, feat))

    def head_copies():
        return (
            (x == 1, remote(block.at[local, 0], hx, (hsent.at[0], hsem.at[0]), beside, feat)),
            ((x == 0) & below, remote(
                block.at[local, 0], hz, (hsent.at[1], hsem.at[1]), tok - 2, feat)),
            ((x == 0) & below, remote(
                block.at[local, 1], hz, (hsent.at[2], hsem.at[1]), tok - 1, feat)),
        )

    carry = {}

    def gradients(k):
        if k == 0:
            starts_of()
        copies["c", k].wait_recv()
        places = lax.broadcasted_iota(jnp.int32, (1, chunk), 1) + (tok * local + k) * chunk
        inside = places.astype(F32) >= spans["start"][k : k + 1]
        now = jnp.where(inside, spans["now"][k : k + 1], 0.0)
        before = jnp.where(inside, 0.0, spans["before"][k : k + 1])
        left = lfin[k]
        weighted = jnp.concatenate([left * now, left * before], axis=0)
        right = rfull[k].reshape(chunk, rank)
        both = times(stack_left(weighted, 1), stack_right(right, 0))
        tail = both[wide:]
        if k:
            settle(k - 1, carry["sum"] + tail)
        else:
            settle(local, tail)
            for condition, copy in head_copies():
                when(condition, copy.start)
        carry["sum"] = both[:wide]
        if k == local - 1:
            settle(k, carry["sum"])

    ways = (DOWN, UP)

    def block_plane(way, step):
        return jnp.clip(plane + step if way == DOWN else plane - step, 0, planes - 1)

    def to_outer(way):
        return (plane == 1 if way == DOWN else plane == planes - 2) if pushed else False

    def sending(way, step, kind=1):
        if way == DOWN:
            base = below & (plane + step < planes)
        else:
            base = above & (plane - step >= 0)
        return base if kind else both(base, no(to_outer(way)))

    def taking(way, step, kind=1):
        base = plane + 1 + step < planes if way == DOWN else plane - 1 - step >= 0
        return base if kind else both(base, no(outer))

    groups = local // 2
    tail_parts = range(pushed, quarters)
    kinds = (0, 1) if pushed else (1,)

    def z_data(at, step, kind, part, count):
        which = pl.ds(pushed, quarters - pushed) if kind else pl.ds(0, pushed)
        if step < 2:
            return gs.at[which, :, seq_rows(at, part, 0, 2 * count), :]
        return gs.at[part, :, seq_rows(at, 0, 0, in_plane), :]

    def z_sems(way, step, kind, part):
        came = zrecv.at[way, kind, part // 2] if step == 0 else (
            zrecv.at[way, kind, groups] if step == 1 else zrecv_late.at[way, step - 2, part])
        return zsent.at[way, kind, step], came

    def z_start(way, step, kind, part, condition):
        count = 2 if step == 1 else 1
        data = z_data(block_plane(way, step), step, kind, part * count, count)
        copy = remote(
            data, data, z_sems(way, step, kind, part),
            tok - 2 if way == DOWN else tok + 2, feat)
        when(condition, copy.start)

    def z_sent():
        for step in range(last_step + 1):
            for way in ways:
                for kind in kinds:
                    if step < 2:
                        data = z_data(block_plane(way, step), step, kind, 0, local)
                    else:
                        at = block_plane(way, step)
                        data = gs.at[pl.ds(pushed, quarters - pushed), :, seq_rows(at, 0, 0, in_plane), :]
                    if step < 2 or kind:
                        await_sent(data, zsent.at[way, kind, step], sending(way, step, kind))

    last_step = max(planes - 2, 0)

    def complete(k):
        copies["x", k].wait_recv()
        if k == local - 1:
            @pl.when(x == 1)
            def _():
                gs[:, :, seq_rows(plane, k, 0), :] += block[local, 1]

            @pl.when(x == 0)
            def _():
                head_copies()[0][1].wait_recv()
                gs[:, :, seq_rows(plane, k, 0), :] += hx[...]

            @pl.when(above)
            def _():
                head_copies()[1][1].wait_recv()
                gs[:, :, seq_rows(plane, k, 1), :] += hz[...]
        if planes > 1:
            for kind in kinds:
                for way in ways:
                    z_start(way, 0, kind, k, sending(way, 0, kind))

    def take(step, kind, part=0):
        if step <= last_step and planes > 1 and kind in kinds:
            for way in ways:
                first, count = (2 * part, 2) if step == 0 else (0, local)
                at = block_plane(way, step + 1)
                data = z_data(at, step, kind, first if step < 2 else part, count)
                came = z_sems(way, step, kind, first if step < 2 else part)[1]
                await_all(data, came, taking(way, step, kind))

    def forward(step, kind, parts, outermost=None):
        if step <= last_step and kind in kinds:
            for part in parts:
                for way in ways:
                    condition = sending(way, step, kind)
                    if outermost is not None:
                        end = to_outer(way)
                        condition = both(condition, end if outermost else no(end))
                    z_start(way, step, kind, part, condition)

    def pass_on(group):
        for kind in kinds:
            take(0, kind, group)
        forward(1, 0, (group,))
        if pushed:
            forward(1, 1, (group,), True)
        else:
            forward(1, 1, (group,))

    def make_mats(target, rows, lanes, value):
        high, low = halves(value)
        count = 2 * store_rows
        target[pl.ds(rows * store_rows, store_rows), lanes] = high
        target[pl.ds(count + rows * store_rows, store_rows), lanes] = low

    def score(target, at, part):
        lines = []
        for line in range(8):
            first = at * in_plane * 8 + line
            for tile in range(tiles):
                lines.append(gs[part, tile, pl.ds(first, in_plane, stride=8), :])
        high, low = halves(jnp.concatenate(lines, axis=1))
        return times_t(
            jnp.concatenate([high, low], axis=0),
            target[:, pl.ds(part * part_lanes, part_lanes)],
        )

    def score_plane(at):
        value = score(mats, at, pushed)
        for part in range(pushed + 1, quarters):
            value += score(mats, at, part)
        sc[at] = value

        def more():
            value = score(mats, at, 0)
            for part in range(1, pushed):
                value += score(mats, at, part)
            sc[at] += value

        if pushed:
            when(no(outer), more)

    def score_guests():
        for step in range(2):
            await_all(guest.at[step], srecv.at[2 + step])
        lanes = pl.ds(0, pushed * part_lanes)
        for step in range(2):
            make_mats(guest_mats, step, lanes, guest[step])
        for at in range(planes):
            value = score(guest_mats, at, 0)
            for part in range(1, pushed):
                value += score(guest_mats, at, part)
            guest_sc[at] = value

    def score_step(step):
        for way in ways:
            when(taking(way, step), lambda way=way: score_plane(block_plane(way, step + 1)))

    def stage_rows(k):
        if 0 <= k < local:
            finish_rows(k)

    def stage_grads(k):
        if 0 <= k < local:
            gradients(k)
            trade(1)

    def stage_complete(k):
        if 0 <= k < local:
            complete(k)

    fold_left()
    fetch_block(1)
    project_in(0)
    pl.semaphore_wait(barrier, met)
    if pushed:
        push_own()
    trade(3)
    for b in range(blocks):
        first = b * span
        send_right(b)
        project_out(b)
        send_left(b)
        pair_right(first)
        if b + 1 < blocks:
            project_in(b + 1)
        else:
            fetch("kept", stored.at[:, column(x, 0, pieces)], kept)
            stage_rows(0)
        pair_left(first)
        for k in range(first + 1, first + span):
            pair_right(k)
            pair_left(k)
        trade(1)
    for k in range(local):
        if k:
            stage_rows(k)
        stage_complete(k - 3)
        if k >= 6 and k % 2 == 0:
            pass_on(k // 2 - 3)
        stage_grads(k)
        if k == 1 and pushed:
            push_given()
    trade(pieces)
    trades_sent()
    rows_sent()
    passed = max(local // 2 - 3, 0)
    loads["kept"].wait()
    make_mats(mats, 0, pl.ds(0, half_lanes), kept[...])
    stage_complete(local - 3)
    if passed < groups - 2:
        pass_on(passed)
        passed += 1
    stage_complete(local - 2)
    stage_complete(local - 1)

    loads["slots"].wait()
    at_row = lax.broadcasted_iota(jnp.int32, (seqs, seqs), 1)
    seq_of = ((at_row // in_plane) * 2 + at_row % 2) * local + (at_row % in_plane) // 2
    by_seq = jnp.where(lax.broadcasted_iota(jnp.int32, (seqs, seqs), 0) == seq_of, 1.0, 0.0)
    by_seq = by_seq.astype(BF16)
    slot = lax.broadcasted_iota(jnp.int32, (seqs, seqs), 0)
    by_slot = times(
        jnp.where(slots[...] == slot, 1.0, 0.0).astype(BF16), by_seq)
    row = lax.broadcasted_iota(jnp.int32, (4 * local, seqs), 0)
    wanted = jnp.zeros((4 * local, seqs), jnp.int32)
    for n, owner in enumerate((tok, beside, partner * 2 + x, partner * 2 + 1 - x)):
        here = (row >= n * local) & (row < (n + 1) * local)
        wanted = jnp.where(here, owner * local + row - n * local, wanted)
    pick = times(
        jnp.where(slots[...] == wanted, 1.0, 0.0).astype(BF16), by_seq).astype(BF16)
    pick = jnp.concatenate([pick, pick], axis=1)

    while passed < groups - 1:
        pass_on(passed)
        passed += 1
    if aside:
        await_all(given.at[:, pl.ds(0, aside * piece)], srecv.at[0], no(outer))
    await_all(given.at[:, pl.ds(aside * piece, (pieces - aside) * piece)], srecv.at[1])

    def given_mats(first, count):
        lanes = pl.ds(first * part_lanes, count * part_lanes)
        make_mats(mats, 1, lanes, given[:, lanes])

    given_mats(pushed, quarters - pushed)
    if pushed:
        when(no(outer), lambda: given_mats(0, pushed))
    score_plane(plane)
    pass_on(groups - 1)
    if pushed:
        forward(1, 1, range(groups), False)
    score_step(0)

    def write(half, part, condition=True):
        lanes = pl.ds(pl.multiple_of(half * half_lanes + part * part_lanes, part_lanes), part_lanes)
        copy = pltpu.make_async_copy(found.at[:, lanes], out.at[:, lanes], wsent.at[0])
        when(condition, copy.start)

    def give(part, n, to, condition):
        lane = part * part_lanes
        there = pl.ds(pl.multiple_of(x * half_lanes + lane, part_lanes), part_lanes)
        sem = psent.at[n, 0 if part < pushed else 1]
        copies["p", n, part] = start(remote(
            picked.at[n, :, pl.ds(lane, part_lanes)], found.at[:, there],
            (sem, precv.at[n, part]), to, feat), condition)

    def rows_for_slots(part):
        count = 4 if part < pushed else 2

        def fill():
            for line in range(8):
                high, low = halves(jnp.concatenate(
                    [gs[part, tile, pl.ds(line, seqs, stride=8), :] for tile in range(tiles)], axis=1))
                taken = times(pick[: count * local], jnp.concatenate([high, low], axis=0))
                lane = part * part_lanes + line * rank
                found[:, pl.ds(pl.multiple_of(x * half_lanes + lane, rank), rank)] = taken[:local]
                for n in range(1, count):
                    picked[n - 1, :, pl.ds(lane, rank)] = taken[n * local : (n + 1) * local]

        condition = no(outer) if part < pushed else True
        when(condition, fill)
        if part < pushed:
            give(part, 1, partner * 2 + x, inner)
            give(part, 2, partner * 2 + 1 - x, inner)
        give(part, 0, beside, condition)
        write(x, part, condition)

    if pushed:
        take(1, 0)
        for part in range(pushed):
            rows_for_slots(part)
    take(1, 1)
    forward(2, 1, tail_parts)
    if last_step > 0:
        score_step(1)
    for step in range(2, last_step):
        for part in tail_parts:
            take(step, 1, part)
        forward(step + 1, 1, tail_parts)
        score_step(step)
    if pushed:
        when(inner, score_guests)
    for part in tail_parts:
        if last_step >= 2:
            take(last_step, 1, part)
        rows_for_slots(part)
    if last_step >= 2:
        score_step(last_step)

    def turn_scores(sums):
        count = 2 * store_rows
        high, low = sums[:, :in_plane], sums[:, in_plane:]
        by_row = (high[:, :, :count] + high[:, :, count:] + low[:, :, :count]).reshape(seqs, count)
        lanes = scored.shape[4]
        placed = jnp.dot(
            by_slot, by_row, precision=lax.Precision.HIGHEST, preferred_element_type=F32)
        if lanes > seqs:
            placed = jnp.concatenate([placed, jnp.zeros((lanes - seqs, count), F32)], axis=0)
        return jnp.transpose(
            jnp.concatenate([placed, jnp.zeros((lanes, 128 - count), F32)], axis=1))

    few = scored.shape[3]
    parts = {}

    def send_scores(kind, own, condition):
        base = partner if kind else plane
        for step in range(2):
            for turn in range(feats):
                if kind or step or turn:
                    to = (feat + turn) % feats
                    parts[kind, step, turn] = start(remote(
                        scored.at[kind, step, to], landed.at[kind, step * feats + turn],
                        (rsent.at[kind], rrecv.at[kind]),
                        base * 2 + (1 - x if step else x), to,
                    ), condition)
        first = 0 if kind else 1
        await_sent(landed.at[kind, pl.ds(first, 2 * feats - first)], rsent.at[kind], condition)

    def place_scores(kind, sums):
        turned = turn_scores(sums)
        for step in range(2):
            for f in range(feats):
                first = (step * feats + f) * few
                scored[kind, step, f] = turned[first : first + few]

    def share_scores():
        if pushed:
            when(inner, lambda: place_scores(1, guest_sc[...]))
            send_scores(1, guest_sc, inner)
        place_scores(0, sc[...])
        send_scores(0, sc, True)

    def sum_scores():
        others = pl.ds(1, 2 * feats - 1)
        await_all(landed.at[0, others], rrecv.at[0])
        summed = scored[0, 0, feat]
        for n in range(1, 2 * feats):
            summed += landed[0, n]
        total[...] = summed[:, :seqs]

        def add_more():
            await_all(landed.at[1], rrecv.at[1])
            more = landed[1, 0]
            for n in range(1, 2 * feats):
                more += landed[1, n]
            total[...] += more[:, :seqs]

        if pushed:
            when(outer, add_more)

    def drain():
        for part in range(quarters):
            arrives = no(outer) if part < pushed else True
            when(arrives, copies["p", 0, part].wait_recv)
            write(1 - x, part, arrives)
        for part in range(pushed):
            for n, half in ((1, x), (2, 1 - x)):
                when(outer, copies["p", n, part].wait_recv)
                write(half, part, outer)
        sum_scores()
        if planes > 1:
            z_sent()
        for kind, first, count in ((0, 0, pushed), (1, pushed, quarters - pushed)):
            lanes = pl.ds(first * part_lanes, count * part_lanes)
            if count:
                await_sent(picked.at[0, :, lanes], psent.at[0, kind], True if kind else no(outer))
                for n in (1, 2):
                    if not kind:
                        await_sent(picked.at[n, :, lanes], psent.at[n, kind], inner)
        for condition, copy in sent:
            when(condition, copy.wait_send)
        for condition, copy in head_copies():
            when(condition, copy.wait_send)
        pltpu.make_async_copy(found, out, wsent.at[0]).wait()

    share_scores()
    drain()


def body(
    activations,
    out_grads,
    proj_in,
    proj_out,
    left_factor,
    right_factor,
    seq_lengths,
    seq_slots,
    stored_grads,
):
    dma = pltpu.SemaphoreType.DMA
    feats, toks = lax.axis_size("feat"), lax.axis_size("tok")
    rank = right_factor.shape[0]
    tok_rows = activations.shape[0]
    seqs = seq_lengths.shape[0]
    local = seqs // toks
    chunk = tok_rows // local
    store_rows, width = stored_grads.shape
    planes, chips = toks // 2, feats // 2
    wide = rank // feats
    quarters = wide // 16
    tiles = rank // 128
    score_rows = store_rows // feats
    lanes = seqs + -seqs % 128
    half = chunk // 2
    steps = max(planes - 1, 1)
    pieces = width // 2 // (2 * rank)
    pushed = pushed_quarters(planes, quarters)
    aside = max(pushed, 1)
    aside_lanes = aside * 8 * rank

    def vmem(*shape, dtype=F32):
        return pltpu.VMEM(shape, dtype)

    scores, own_rows = pl.pallas_call(
        functools.partial(kernel, (toks, feats, local, chunk, rank, seqs, store_rows)),
        out_shape=[
            jax.ShapeDtypeStruct((score_rows, seqs), F32),
            jax.ShapeDtypeStruct((local, width), F32),
        ],
        in_specs=[ANY] * 9,
        out_specs=[VMEM, ANY],
        scratch_shapes=[
            vmem(*out_grads.shape, dtype=BF16),
            vmem(*activations.shape, dtype=BF16),
            vmem(*proj_out.shape, dtype=BF16),
            vmem(*proj_in.shape, dtype=BF16),
            vmem(rank, rank),
            vmem(rank, rank),
            vmem(1, seqs, dtype=jnp.int32),
            vmem(1, seqs, dtype=jnp.int32),
            vmem(2, rank, rank, dtype=BF16),
            vmem(3 * rank, rank, dtype=BF16),
            vmem(2, *proj_out.shape, dtype=BF16),
            vmem(local, 2, chips, wide, chunk),
            vmem(local, chips, wide, chunk),
            vmem(local, chips, wide, chunk),
            vmem(local, chips - 1, wide, chunk),
            vmem(local, wide, chunk),
            vmem(local, 2, half, rank),
            vmem(local, half, rank),
            vmem(local, half, rank),
            vmem(local, chips - 1, half, rank),
            vmem(local, 2, half, rank),
            vmem(local + 1, 2, quarters, tiles, 8, 128),
            vmem(quarters, tiles, 8, 128),
            vmem(quarters, tiles, 8, 128),
            vmem(quarters, tiles, seqs * 8, 128),
            vmem(store_rows, width // 2),
            vmem(store_rows, width // 2),
            vmem(2, store_rows, aside_lanes),
            vmem(4 * store_rows, width // 2, dtype=BF16),
            vmem(4 * store_rows, aside_lanes, dtype=BF16),
            vmem(planes, 4 * local, 4 * store_rows),
            vmem(planes, 4 * local, 4 * store_rows),
            vmem(local, width),
            vmem(3, local, width // 2),
            vmem(2, 2, feats, score_rows, lanes),
            vmem(2, 2 * feats, score_rows, lanes),
            dma((2 * (local // 2 if local % 2 == 0 else local) + 7,)),
            dma((2, local)),
            dma((2, local, chips - 1)),
            dma((local,)),
            dma((local,)),
            dma((2,)),
            dma((2, 2, local // 2 + 1)),
            dma((2, max(steps - 2, 1), quarters)),
            dma((4,)),
            dma((3, quarters)),
            dma((2,)),
            dma((2,)),
            dma((2, chips - 1)),
            dma((1,)),
            dma((1,)),
            dma((3,)),
            dma((2, 2, steps)),
            dma((4,)),
            dma((3, 2)),
            dma((2,)),
            dma((1,)),
        ],
        compiler_params=pltpu.CompilerParams(
            collective_id=0, has_side_effects=True, vmem_limit_bytes=60 << 20
        ),
        name="influence",
    )(
        out_grads, activations, proj_out, proj_in, left_factor, right_factor,
        seq_lengths.reshape(1, seqs), seq_slots.reshape(1, seqs), stored_grads,
    )
    return scores, own_rows


def solution(mesh):
    placed = (
        P("tok", "feat"),
        P("tok", "feat"),
        P("feat", None),
        P("feat", None),
        P(),
        P(),
        P(),
        P(),
        P("tok", "feat"),
    )
    return jax.shard_map(
        body,
        mesh=mesh,
        in_specs=placed,
        out_specs=(P(("tok", "feat"), None), P("tok", "feat")),
        check_vma=False,
    )
```

time: 79.1 us -> 70.4 us (0.89)
  Pallas kernels: 75.2 us -> 66.5 us
    pallas_call x1, Pallas kernels: 75.2 us -> 66.5 us  [body(): pl.pallas_call(functools.partial(kernel, (toks, feats, local, chunk, rank...]
where the time goes in v2:
time: 70.4 us; the launch traced here: 70.3 us
  Pallas kernels  66.5 us (94%)
  local copies, waits for them, and re-layouts  3.13 us (4%)
    pallas_call x1, Pallas kernels, body(): pl.pallas_call(functools.partial(kernel, (toks, feats, local, chunk, rank...  66.5 us
    unnamed x2, local copies, waits for them, and re-layouts  3.13 us

profile of v2, /device:TPU:0, one launch (start us, length us, event | category | flops | bytes accessed | tf_op | source)
XLA Modules:
  0.0 70.3 jit_solution(3901824013037465616)
XLA Ops:
  0.6 66.5 %influence.1 = (f32[8,64]{1,0:T(8,128)}, f32[8,16384]{1,0:T(8,128)}) custom-call(bf16[1024,2048]{1,0:T(8,128)(2,1)} %refs_0_.1, bf16[1024,7168]{1,0:T(8,128)(2,1)} %refs_1_.1, bf16[2048,256]{1,0:T(8,128)(2,1)} %refs_2_.1, bf16[7168,256]{1,0:T(8,128)(2,1)} %refs_3_.1, f32[256,256]{1,0:T(8,128)} %refs_4_.1, f32[256,256]{1,0:T(8,128)} %refs_5_.1, ...), custom_call_target="tpu_custom_call" | custom-call | tf_op jit(solution)/shard_map/influence/pallas_call | solution.py:793
  67.1 1.3 %copy.13 = f32[8,64]{1,0:T(8,128)} copy(f32[8,64]{1,0:T(8,128)} %get-tuple-element.4) | data formatting | bytes 4096
  68.4 1.9 %copy.14 = f32[8,16384]{1,0:T(8,128)} copy(f32[8,16384]{1,0:T(8,128)} %get-tuple-element.5) | data formatting | bytes 1048576

commit v3 on v2

--- a/solution.py
+++ b/solution.py
@@ -42,7 +42,7 @@
 
 
 def pushed_quarters(planes, quarters):
-    return quarters // 4 if planes == 4 else 0
+    return quarters // 2 if planes == 4 else 0
 
 
 def both(first, second):
@@ -74,9 +74,9 @@
     rp, ra, ry, rb, rfull = refs[27:32]
     block, hx, hz, gs = refs[32:36]
     kept, given, guest, mats, guest_mats, sc, guest_sc = refs[36:43]
-    found, picked, scored, landed = refs[43:47]
-    load, asem, bsem, csem, xsem, hsem, zrecv, zrecv_late, srecv, precv, rrecv = refs[47:58]
-    asent, bsent, csent, xsent, hsent, zsent, ssent, psent, rsent, wsent = refs[58:]
+    picked, scored, landed = refs[43:46]
+    load, asem, bsem, csem, xsem, hsem, zrecv, zlast, srecv, precv, rrecv = refs[46:57]
+    asent, bsent, csent, xsent, hsent, zsent, ssent, psent, rsent = refs[57:]
 
     tok, feat = lax.axis_index("tok"), lax.axis_index("feat")
     plane, x = tok // 2, tok % 2
@@ -119,11 +119,13 @@
     def fetch_block(b):
         if b < blocks:
             rows = pl.ds(b * tall, tall)
+            if b:
+                fetch(("o", b), out_rows.at[rows], lhs_o.at[rows])
             fetch(("i", b), in_rows.at[rows], lhs_i.at[rows])
-            fetch(("o", b), out_rows.at[rows], lhs_o.at[rows])
 
     fetch("left", left_hbm, left_f)
     fetch("out", out_mat, rhs_o)
+    fetch(("o", 0), out_rows.at[pl.ds(0, tall)], lhs_o.at[pl.ds(0, tall)])
     fetch("in", in_mat, rhs_i)
     fetch_block(0)
     fetch("lens", lens_hbm, lens)
@@ -189,13 +191,18 @@
         start(copy, outer)
         await_sent(stored.at[:, column(x, 0, aside)], ssent.at[2], outer)
 
-    def push_given():
-        lanes = pl.ds(0, aside * piece)
-        await_all(given.at[:, lanes], srecv.at[0], outer)
-        copy = remote(
-            given.at[:, lanes], guest.at[1], (ssent.at[3], srecv.at[3]), partner * 2 + x, feat)
-        start(copy, outer)
-        await_sent(given.at[:, lanes], ssent.at[3], outer)
+    batches = 4 if pushed else 0
+    batch = aside // 4
+
+    def batch_lanes(n):
+        return pl.ds(n * batch * piece, batch * piece)
+
+    def push_given(n):
+        lanes = batch_lanes(n)
+        await_all(given.at[:, lanes], srecv.at[4 + n], outer)
+        start(remote(
+            given.at[:, lanes], guest.at[1, :, lanes], (ssent.at[3], srecv.at[3]),
+            partner * 2 + x, feat), outer)
 
     def trade(count):
         for _ in range(count):
@@ -204,12 +211,13 @@
                 kind = 0 if n < aside else 1
                 trades.append(start(remote(
                     stored.at[:, column(1 - x, n)], given.at[:, pl.ds(n * piece, piece)],
-                    (ssent.at[kind], srecv.at[kind]), beside, feat,
+                    (ssent.at[kind], srecv.at[1 if kind else 4 + n // batch]), beside, feat,
                 )))
 
     def trades_sent():
         if aside:
             await_sent(stored.at[:, column(1 - x, 0, aside)], ssent.at[0])
+            await_sent(given.at[:, pl.ds(0, aside * piece)], ssent.at[3], outer)
         await_sent(stored.at[:, column(1 - x, aside, pieces - aside)], ssent.at[1])
 
     copies = {}
@@ -254,6 +262,8 @@
         if b == 0:
             loads["in"].wait()
         loads["i", b].wait()
+        if b == 0:
+            fetch_block(1)
         fetch_block(b + 2)
         own = [lhs_i[pl.ds((b * span + n) * chunk, chunk), :] for n in range(span)]
         for n, sums in enumerate([times(rows, rhs_i[...]) for rows in own]):
@@ -383,35 +393,27 @@
     tail_parts = range(pushed, quarters)
     kinds = (0, 1) if pushed else (1,)
 
-    def z_data(at, step, kind, part, count):
+    def z_data(at, kind, first, count):
         which = pl.ds(pushed, quarters - pushed) if kind else pl.ds(0, pushed)
-        if step < 2:
-            return gs.at[which, :, seq_rows(at, part, 0, 2 * count), :]
-        return gs.at[part, :, seq_rows(at, 0, 0, in_plane), :]
-
-    def z_sems(way, step, kind, part):
-        came = zrecv.at[way, kind, part // 2] if step == 0 else (
-            zrecv.at[way, kind, groups] if step == 1 else zrecv_late.at[way, step - 2, part])
-        return zsent.at[way, kind, step], came
-
-    def z_start(way, step, kind, part, condition):
-        count = 2 if step == 1 else 1
-        data = z_data(block_plane(way, step), step, kind, part * count, count)
+        return gs.at[which, :, seq_rows(at, first, 0, 2 * count), :]
+
+    def z_start(way, step, kind, first, count, part=None):
+        data = z_data(block_plane(way, step), kind, first, count)
+        came = zrecv.at[way, kind, step, first // 2]
+        if part is not None:
+            data = gs.at[part, :, seq_rows(block_plane(way, step), first, 0, 2 * count), :]
+            came = zlast.at[way, part]
         copy = remote(
-            data, data, z_sems(way, step, kind, part),
+            data, data, (zsent.at[way, kind, step], came),
             tok - 2 if way == DOWN else tok + 2, feat)
-        when(condition, copy.start)
+        when(sending(way, step, kind), copy.start)
 
     def z_sent():
         for step in range(last_step + 1):
             for way in ways:
                 for kind in kinds:
-                    if step < 2:
-                        data = z_data(block_plane(way, step), step, kind, 0, local)
-                    else:
-                        at = block_plane(way, step)
-                        data = gs.at[pl.ds(pushed, quarters - pushed), :, seq_rows(at, 0, 0, in_plane), :]
-                    if step < 2 or kind:
+                    if kind or step < 2:
+                        data = z_data(block_plane(way, step), kind, 0, local)
                         await_sent(data, zsent.at[way, kind, step], sending(way, step, kind))
 
     last_step = max(planes - 2, 0)
@@ -435,35 +437,37 @@
         if planes > 1:
             for kind in kinds:
                 for way in ways:
-                    z_start(way, 0, kind, k, sending(way, 0, kind))
-
-    def take(step, kind, part=0):
-        if step <= last_step and planes > 1 and kind in kinds:
-            for way in ways:
-                first, count = (2 * part, 2) if step == 0 else (0, local)
-                at = block_plane(way, step + 1)
-                data = z_data(at, step, kind, first if step < 2 else part, count)
-                came = z_sems(way, step, kind, first if step < 2 else part)[1]
-                await_all(data, came, taking(way, step, kind))
-
-    def forward(step, kind, parts, outermost=None):
-        if step <= last_step and kind in kinds:
-            for part in parts:
-                for way in ways:
-                    condition = sending(way, step, kind)
-                    if outermost is not None:
-                        end = to_outer(way)
-                        condition = both(condition, end if outermost else no(end))
-                    z_start(way, step, kind, part, condition)
-
-    def pass_on(group):
-        for kind in kinds:
-            take(0, kind, group)
-        forward(1, 0, (group,))
-        if pushed:
-            forward(1, 1, (group,), True)
-        else:
-            forward(1, 1, (group,))
+                    z_start(way, 0, kind, k, 1)
+
+    def take(step, kind, group):
+        for way in ways:
+            data = z_data(block_plane(way, step + 1), kind, 2 * group, 2)
+            await_all(data, zrecv.at[way, kind, step, group], taking(way, step, kind))
+
+    whole_groups = groups - 1 if last_step >= 2 else groups
+
+    def pass_on(step, group, only=kinds):
+        if planes > 1 and step <= last_step:
+            for kind in only:
+                if kind or step < 2:
+                    take(step, kind, group)
+                if step < last_step and (kind or step + 1 < 2):
+                    split = step + 1 == last_step and last_step >= 2
+                    for way in ways:
+                        if not split or group < whole_groups:
+                            z_start(way, step + 1, kind, 2 * group, 2)
+                    if split and group == groups - 1:
+                        for part in tail_parts:
+                            for way in ways:
+                                z_start(way, step + 1, kind, 2 * whole_groups,
+                                        local - 2 * whole_groups, part)
+
+    def take_last(part):
+        first = 2 * whole_groups
+        for way in ways:
+            at = block_plane(way, last_step + 1)
+            data = gs.at[part, :, seq_rows(at, first, 0, 2 * (local - first)), :]
+            await_all(data, zlast.at[way, part], taking(way, last_step))
 
     def make_mats(target, rows, lanes, value):
         high, low = halves(value)
@@ -521,56 +525,69 @@
     def stage_grads(k):
         if 0 <= k < local:
             gradients(k)
-            trade(1)
+            if k % 2 and 1 < k < local - 2:
+                trade(1)
 
     def stage_complete(k):
         if 0 <= k < local:
             complete(k)
 
     fold_left()
-    fetch_block(1)
-    project_in(0)
+    project_out(0)
     pl.semaphore_wait(barrier, met)
+    send_left(0)
     if pushed:
         push_own()
     trade(3)
+    early = min(2, local) if blocks >= 3 else 0
     for b in range(blocks):
-        first = b * span
+        chunks = range(b * span, b * span + span)
+        if b == 0:
+            for k in chunks:
+                pair_left(k)
+        project_in(b)
         send_right(b)
-        project_out(b)
-        send_left(b)
-        pair_right(first)
+        if b:
+            for k in chunks:
+                pair_left(k)
+        if b == 1:
+            trade(2)
+        if b == blocks - 2 and early:
+            stage_rows(0)
         if b + 1 < blocks:
-            project_in(b + 1)
+            project_out(b + 1)
+            send_left(b + 1)
         else:
             fetch("kept", stored.at[:, column(x, 0, pieces)], kept)
-            stage_rows(0)
-        pair_left(first)
-        for k in range(first + 1, first + span):
+        for k in chunks:
             pair_right(k)
-            pair_left(k)
-        trade(1)
-    for k in range(local):
-        if k:
-            stage_rows(k)
+        if b == blocks - 2 and early:
+            stage_grads(0)
+            stage_rows(1)
+    if early:
+        stage_grads(1)
+    passed = 0
+    for k in range(early, local):
         stage_complete(k - 3)
-        if k >= 6 and k % 2 == 0:
-            pass_on(k // 2 - 3)
+        stage_rows(k)
         stage_grads(k)
-        if k == 1 and pushed:
-            push_given()
+        if k >= 5 and k % 2:
+            pass_on(0, (k - 5) // 2)
+            passed = (k - 5) // 2 + 1
     trade(pieces)
     trades_sent()
     rows_sent()
-    passed = max(local // 2 - 3, 0)
+    stage_complete(local - 3)
     loads["kept"].wait()
     make_mats(mats, 0, pl.ds(0, half_lanes), kept[...])
-    stage_complete(local - 3)
-    if passed < groups - 2:
-        pass_on(passed)
-        passed += 1
+    for group in range(passed, groups - 2):
+        pass_on(0, group)
+    passed = max(passed, groups - 2)
     stage_complete(local - 2)
     stage_complete(local - 1)
+    for n in range(batches):
+        push_given(n)
+    pass_on(1, 0, (1,))
 
     loads["slots"].wait()
     at_row = lax.broadcasted_iota(jnp.int32, (seqs, seqs), 1)
@@ -589,81 +606,43 @@
         jnp.where(slots[...] == wanted, 1.0, 0.0).astype(BF16), by_seq).astype(BF16)
     pick = jnp.concatenate([pick, pick], axis=1)
 
-    while passed < groups - 1:
-        pass_on(passed)
-        passed += 1
-    if aside:
-        await_all(given.at[:, pl.ds(0, aside * piece)], srecv.at[0], no(outer))
-    await_all(given.at[:, pl.ds(aside * piece, (pieces - aside) * piece)], srecv.at[1])
+    for group in range(passed, groups):
+        pass_on(0, group)
+        pass_on(1, group - 1, (1,))
 
     def given_mats(first, count):
         lanes = pl.ds(first * part_lanes, count * part_lanes)
         make_mats(mats, 1, lanes, given[:, lanes])
-
-    given_mats(pushed, quarters - pushed)
-    if pushed:
-        when(no(outer), lambda: given_mats(0, pushed))
-    score_plane(plane)
-    pass_on(groups - 1)
-    if pushed:
-        forward(1, 1, range(groups), False)
-    score_step(0)
-
-    def write(half, part, condition=True):
-        lanes = pl.ds(pl.multiple_of(half * half_lanes + part * part_lanes, part_lanes), part_lanes)
-        copy = pltpu.make_async_copy(found.at[:, lanes], out.at[:, lanes], wsent.at[0])
-        when(condition, copy.start)
 
     def give(part, n, to, condition):
         lane = part * part_lanes
         there = pl.ds(pl.multiple_of(x * half_lanes + lane, part_lanes), part_lanes)
         sem = psent.at[n, 0 if part < pushed else 1]
         copies["p", n, part] = start(remote(
-            picked.at[n, :, pl.ds(lane, part_lanes)], found.at[:, there],
+            picked.at[n, :, pl.ds(lane, part_lanes)], out.at[:, there],
             (sem, precv.at[n, part]), to, feat), condition)
 
-    def rows_for_slots(part):
+    def fill_rows(part):
         count = 4 if part < pushed else 2
-
-        def fill():
-            for line in range(8):
-                high, low = halves(jnp.concatenate(
-                    [gs[part, tile, pl.ds(line, seqs, stride=8), :] for tile in range(tiles)], axis=1))
-                taken = times(pick[: count * local], jnp.concatenate([high, low], axis=0))
-                lane = part * part_lanes + line * rank
-                found[:, pl.ds(pl.multiple_of(x * half_lanes + lane, rank), rank)] = taken[:local]
-                for n in range(1, count):
-                    picked[n - 1, :, pl.ds(lane, rank)] = taken[n * local : (n + 1) * local]
-
-        condition = no(outer) if part < pushed else True
-        when(condition, fill)
+        for line in range(8):
+            high, low = halves(jnp.concatenate(
+                [gs[part, tile, pl.ds(line, seqs, stride=8), :] for tile in range(tiles)], axis=1))
+            taken = times(pick[: count * local], jnp.concatenate([high, low], axis=0))
+            lane = part * part_lanes + line * rank
+            out[:, pl.ds(pl.multiple_of(x * half_lanes + lane, rank), rank)] = taken[:local]
+            for n in range(1, count):
+                picked[n - 1, :, pl.ds(lane, rank)] = taken[n * local : (n + 1) * local]
+
+    def hand_rows(part, condition):
         if part < pushed:
             give(part, 1, partner * 2 + x, inner)
             give(part, 2, partner * 2 + 1 - x, inner)
         give(part, 0, beside, condition)
-        write(x, part, condition)
-
-    if pushed:
-        take(1, 0)
-        for part in range(pushed):
-            rows_for_slots(part)
-    take(1, 1)
-    forward(2, 1, tail_parts)
-    if last_step > 0:
-        score_step(1)
-    for step in range(2, last_step):
-        for part in tail_parts:
-            take(step, 1, part)
-        forward(step + 1, 1, tail_parts)
-        score_step(step)
-    if pushed:
-        when(inner, score_guests)
-    for part in tail_parts:
-        if last_step >= 2:
-            take(last_step, 1, part)
-        rows_for_slots(part)
-    if last_step >= 2:
-        score_step(last_step)
+
+    def rows_for_slots(part):
+        condition = no(outer) if part < pushed else True
+        when(condition, lambda: fill_rows(part))
+        hand_rows(part, condition)
 
     def turn_scores(sums):
         count = 2 * store_rows
@@ -701,12 +680,52 @@
                 first = (step * feats + f) * few
                 scored[kind, step, f] = turned[first : first + few]
 
+    def share_guests():
+        when(inner, lambda: place_scores(1, guest_sc[...]))
+        send_scores(1, guest_sc, inner)
+
     def share_scores():
-        if pushed:
-            when(inner, lambda: place_scores(1, guest_sc[...]))
-            send_scores(1, guest_sc, inner)
         place_scores(0, sc[...])
         send_scores(0, sc, True)
+
+    if pushed:
+        for group in range(groups):
+            pass_on(1, group, (0,))
+        for part in range(pushed):
+            rows_for_slots(part)
+        pass_on(1, groups - 1, (1,))
+        when(inner, score_guests)
+        share_guests()
+        when(inner, lambda: [fill_rows(part) for part in tail_parts] and None)
+        for part in tail_parts:
+            hand_rows(part, inner)
+    else:
+        pass_on(1, groups - 1, (1,))
+    for n in range(batches):
+        await_all(given.at[:, batch_lanes(n)], srecv.at[4 + n], no(outer))
+    await_all(given.at[:, pl.ds(aside * piece, (pieces - aside) * piece)], srecv.at[1])
+    given_mats(pushed, quarters - pushed)
+    if pushed:
+        when(no(outer), lambda: given_mats(0, pushed))
+    score_plane(plane)
+    score_step(0)
+    if last_step > 0:
+        score_step(1)
+    for step in range(2, last_step + 1):
+        for group in range(groups if step < last_step else whole_groups):
+            pass_on(step, group)
+        if step < last_step:
+            score_step(step)
+    for part in tail_parts:
+        if last_step >= 2:
+            take_last(part)
+        if pushed:
+            when(outer, lambda part=part: fill_rows(part))
+            hand_rows(part, outer)
+        else:
+            rows_for_slots(part)
+    if last_step >= 2:
+        score_step(last_step)
 
     def sum_scores():
         others = pl.ds(1, 2 * feats - 1)
@@ -730,11 +749,9 @@
         for part in range(quarters):
             arrives = no(outer) if part < pushed else True
             when(arrives, copies["p", 0, part].wait_recv)
-            write(1 - x, part, arrives)
         for part in range(pushed):
-            for n, half in ((1, x), (2, 1 - x)):
+            for n in (1, 2):
                 when(outer, copies["p", n, part].wait_recv)
-                write(half, part, outer)
         sum_scores()
         if planes > 1:
             z_sent()
@@ -749,7 +766,6 @@
             when(condition, copy.wait_send)
         for condition, copy in head_copies():
             when(condition, copy.wait_send)
-        pltpu.make_async_copy(found, out, wsent.at[0]).wait()
 
     share_scores()
     drain()
@@ -793,11 +809,11 @@
     scores, own_rows = pl.pallas_call(
         functools.partial(kernel, (toks, feats, local, chunk, rank, seqs, store_rows)),
         out_shape=[
-            jax.ShapeDtypeStruct((score_rows, seqs), F32),
-            jax.ShapeDtypeStruct((local, width), F32),
+            pltpu.VMEM((score_rows, seqs), F32),
+            pltpu.VMEM((local, width), F32),
         ],
         in_specs=[ANY] * 9,
-        out_specs=[VMEM, ANY],
+        out_specs=[VMEM, VMEM],
         scratch_shapes=[
             vmem(*out_grads.shape, dtype=BF16),
             vmem(*activations.shape, dtype=BF16),
@@ -831,7 +847,6 @@
             vmem(4 * store_rows, aside_lanes, dtype=BF16),
             vmem(planes, 4 * local, 4 * store_rows),
             vmem(planes, 4 * local, 4 * store_rows),
-            vmem(local, width),
             vmem(3, local, width // 2),
             vmem(2, 2, feats, score_rows, lanes),
             vmem(2, 2 * feats, score_rows, lanes),
@@ -841,9 +856,9 @@
             dma((local,)),
             dma((local,)),
             dma((2,)),
-            dma((2, 2, local // 2 + 1)),
-            dma((2, max(steps - 2, 1), quarters)),
-            dma((4,)),
+            dma((2, 2, steps, (local + 1) // 2)),
+            dma((2, quarters)),
+            dma((8,)),
             dma((3, quarters)),
             dma((2,)),
             dma((2,)),
@@ -855,7 +870,6 @@
             dma((4,)),
             dma((3, 2)),
             dma((2,)),
-            dma((1,)),
         ],
         compiler_params=pltpu.CompilerParams(
             collective_id=0, has_side_effects=True, vmem_limit_bytes=60 << 20

time: 70.4 us -> 63 us (0.89)
  Pallas kernels: 66.5 us -> 60.8 us
  local copies, waits for them, and re-layouts: 3.13 us -> 1.39 us
    pallas_call x1, Pallas kernels: 66.5 us -> 60.8 us  [body(): pl.pallas_call(functools.partial(kernel, (toks, feats, local, chunk, rank...]
    unnamed x2, local copies, waits for them, and re-layouts: 3.13 us -> 1.39 us
where the time goes in v3:
time: 63 us; the launch traced here: 62.8 us
  Pallas kernels  60.8 us (97%)
  local copies, waits for them, and re-layouts  1.39 us (2%)
  between operations  0.64 us (1%)
    pallas_call x1, Pallas kernels, body(): pl.pallas_call(functools.partial(kernel, (toks, feats, local, chunk, rank...  60.8 us
    unnamed x2, local copies, waits for them, and re-layouts  1.39 us

profile of v3, /device:TPU:0, one launch (start us, length us, event | category | flops | bytes accessed | tf_op | source)
XLA Modules:
  0.0 62.8 jit_solution(6511151064787654821)
XLA Ops:
  0.6 60.8 %influence.1 = (f32[8,64]{1,0:T(8,128)S(1)}, f32[8,16384]{1,0:T(8,128)S(1)}) custom-call(bf16[1024,2048]{1,0:T(8,128)(2,1)} %refs_0_.1, bf16[1024,7168]{1,0:T(8,128)(2,1)} %refs_1_.1, bf16[2048,256]{1,0:T(8,128)(2,1)} %refs_2_.1, bf16[7168,256]{1,0:T(8,128)(2,1)} %refs_3_.1, f32[256,256]{1,0:T(8,128)} %refs_4_.1, f32[256,256]{1,0:T(8,128)} %refs_5_.1, ...), custom_call_target="tpu_custom_call" | custom-call | tf_op jit(solution)/shard_map/influence/pallas_call | solution.py:809
  61.4 0.6 copy.13
  62.0 0.8 %copy.14 = f32[8,16384]{1,0:T(8,128)} copy(f32[8,16384]{1,0:T(8,128)S(1)} %get-tuple-element.3) | data formatting | bytes 1048576

commit v4 on v3

--- a/solution.py
+++ b/solution.py
@@ -550,8 +550,6 @@
         if b:
             for k in chunks:
                 pair_left(k)
-        if b == 1:
-            trade(2)
         if b == blocks - 2 and early:
             stage_rows(0)
         if b + 1 < blocks:
@@ -559,19 +557,19 @@
             send_left(b + 1)
         else:
             fetch("kept", stored.at[:, column(x, 0, pieces)], kept)
+            if early:
+                stage_grads(1)
         for k in chunks:
             pair_right(k)
         if b == blocks - 2 and early:
             stage_grads(0)
             stage_rows(1)
-    if early:
-        stage_grads(1)
     passed = 0
     for k in range(early, local):
+        stage_rows(k)
         stage_complete(k - 3)
-        stage_rows(k)
         stage_grads(k)
-        if k >= 5 and k % 2:
+        if k >= 5 and k % 2 and k < local - 1:
             pass_on(0, (k - 5) // 2)
             passed = (k - 5) // 2 + 1
     trade(pieces)
@@ -580,11 +578,11 @@
     stage_complete(local - 3)
     loads["kept"].wait()
     make_mats(mats, 0, pl.ds(0, half_lanes), kept[...])
+    stage_complete(local - 2)
+    stage_complete(local - 1)
     for group in range(passed, groups - 2):
         pass_on(0, group)
     passed = max(passed, groups - 2)
-    stage_complete(local - 2)
-    stage_complete(local - 1)
     for n in range(batches):
         push_given(n)
     pass_on(1, 0, (1,))
@@ -691,9 +689,9 @@
     if pushed:
         for group in range(groups):
             pass_on(1, group, (0,))
+        pass_on(1, groups - 1, (1,))
         for part in range(pushed):
             rows_for_slots(part)
-        pass_on(1, groups - 1, (1,))
         when(inner, score_guests)
         share_guests()
         when(inner, lambda: [fill_rows(part) for part in tail_parts] and None)

time: 63 us -> 59.4 us (0.943)
  Pallas kernels: 60.8 us -> 57.3 us
    pallas_call x1, Pallas kernels: 60.8 us -> 57.3 us  [body(): pl.pallas_call(functools.partial(kernel, (toks, feats, local, chunk, rank...]
where the time goes in v4:
time: 59.4 us; the launch traced here: 59.3 us
  Pallas kernels  57.3 us (96%)
  local copies, waits for them, and re-layouts  1.39 us (2%)
  between operations  0.64 us (1%)
    pallas_call x1, Pallas kernels, body(): pl.pallas_call(functools.partial(kernel, (toks, feats, local, chunk, rank...  57.3 us
    unnamed x2, local copies, waits for them, and re-layouts  1.39 us

profile of v4, /device:TPU:0, one launch (start us, length us, event | category | flops | bytes accessed | tf_op | source)
XLA Modules:
  0.0 59.3 jit_solution(8760329665596905582)
XLA Ops:
  0.6 57.3 %influence.1 = (f32[8,64]{1,0:T(8,128)S(1)}, f32[8,16384]{1,0:T(8,128)S(1)}) custom-call(bf16[1024,2048]{1,0:T(8,128)(2,1)} %refs_0_.1, bf16[1024,7168]{1,0:T(8,128)(2,1)} %refs_1_.1, bf16[2048,256]{1,0:T(8,128)(2,1)} %refs_2_.1, bf16[7168,256]{1,0:T(8,128)(2,1)} %refs_3_.1, f32[256,256]{1,0:T(8,128)} %refs_4_.1, f32[256,256]{1,0:T(8,128)} %refs_5_.1, ...), custom_call_target="tpu_custom_call" | custom-call | tf_op jit(solution)/shard_map/influence/pallas_call | solution.py:807
  57.9 0.6 %copy.13 = f32[8,64]{1,0:T(8,128)} copy(f32[8,64]{1,0:T(8,128)S(1)} %get-tuple-element.2) | data formatting | bytes 4096
  58.5 0.8 %copy.14 = f32[8,16384]{1,0:T(8,128)} copy(f32[8,16384]{1,0:T(8,128)S(1)} %get-tuple-element.3) | data formatting | bytes 1048576

commit v5 on v4

--- a/solution.py
+++ b/solution.py
@@ -75,8 +75,8 @@
     block, hx, hz, gs = refs[32:36]
     kept, given, guest, mats, guest_mats, sc, guest_sc = refs[36:43]
     picked, scored, landed = refs[43:46]
-    load, asem, bsem, csem, xsem, hsem, zrecv, zlast, srecv, precv, rrecv = refs[46:57]
-    asent, bsent, csent, xsent, hsent, zsent, ssent, psent, rsent = refs[57:]
+    load, asem, bsem, csem, xsem, hsem, zpushed, zkept, zlast, srecv, precv, rrecv = refs[46:58]
+    asent, bsent, csent, xsent, hsent, zsent, ssent, psent, rsent = refs[58:]
 
     tok, feat = lax.axis_index("tok"), lax.axis_index("feat")
     plane, x = tok // 2, tok % 2
@@ -248,10 +248,11 @@
     def send_left(b):
         for k in range(b * span, b * span + span):
             copies["a", 0, k] = start(remote(
-                lp.at[k, 1 - c], la.at[k], (asent.at[0], asem.at[0, k]), tok, mate))
+                lp.at[k, 1 - c], la.at[k], (asent.at[0], asem.at[0, b]), tok, mate))
 
     def pair_left(k):
-        copies["a", 0, k].wait_recv()
+        if k % span == 0:
+            await_all(la.at[pl.ds(k, span)], asem.at[0, k // span])
         ly[k] = lp[k, c] + la[k]
         for n, other in enumerate(across):
             copies["b", 0, k, n] = start(remote(
@@ -272,10 +273,11 @@
     def send_right(b):
         for k in range(b * span, b * span + span):
             copies["a", 1, k] = start(remote(
-                rp.at[k, 1 - c], ra.at[k], (asent.at[1], asem.at[1, k]), tok, mate))
+                rp.at[k, 1 - c], ra.at[k], (asent.at[1], asem.at[1, b]), tok, mate))
 
     def pair_right(k):
-        copies["a", 1, k].wait_recv()
+        if k % span == 0:
+            await_all(ra.at[pl.ds(k, span)], asem.at[1, k // span])
         ry[k] = rp[k, c] + ra[k]
         for n, other in enumerate(across):
             copies["b", 1, k, n] = start(remote(
@@ -335,6 +337,8 @@
             copies["x", k] = start(remote(
                 block.at[k, 1 - x], gs.at[:, :, seq_rows(plane, k, x), :],
                 (xsent.at[0], xsem.at[k]), beside, feat))
+            if k < local - 1:
+                z_own(k, x)
 
     def head_copies():
         return (
@@ -399,7 +403,7 @@
 
     def z_start(way, step, kind, first, count, part=None):
         data = z_data(block_plane(way, step), kind, first, count)
-        came = zrecv.at[way, kind, step, first // 2]
+        came = came_by(way, kind, step, first // 2)
         if part is not None:
             data = gs.at[part, :, seq_rows(block_plane(way, step), first, 0, 2 * count), :]
             came = zlast.at[way, part]
@@ -408,6 +412,27 @@
             tok - 2 if way == DOWN else tok + 2, feat)
         when(sending(way, step, kind), copy.start)
 
+    def came_by(way, kind, step, group):
+        if kind:
+            return zkept.at[way, step, group]
+        return zpushed.at[way, groups if step else group]
+
+    def take_pushed():
+        for way in ways:
+            data = z_data(block_plane(way, 2), 0, 0, local)
+            await_all(data, came_by(way, 0, 1, 0), taking(way, 1, 0))
+
+    def z_own(number, side):
+        if planes > 1:
+            for kind in kinds:
+                which = pl.ds(pushed, quarters - pushed) if kind else pl.ds(0, pushed)
+                data = gs.at[which, :, seq_rows(plane, number, side), :]
+                for way in ways:
+                    copy = remote(
+                        data, data, (zsent.at[way, kind, 0], came_by(way, kind, 0, number // 2)),
+                        tok - 2 if way == DOWN else tok + 2, feat)
+                    when(sending(way, 0, kind), copy.start)
+
     def z_sent():
         for step in range(last_step + 1):
             for way in ways:
@@ -434,15 +459,14 @@
             def _():
                 head_copies()[1][1].wait_recv()
                 gs[:, :, seq_rows(plane, k, 1), :] += hz[...]
-        if planes > 1:
-            for kind in kinds:
-                for way in ways:
-                    z_start(way, 0, kind, k, 1)
+        z_own(k, 1 - x)
+        if k == local - 1:
+            z_own(k, x)
 
     def take(step, kind, group):
         for way in ways:
             data = z_data(block_plane(way, step + 1), kind, 2 * group, 2)
-            await_all(data, zrecv.at[way, kind, step, group], taking(way, step, kind))
+            await_all(data, came_by(way, kind, step, group), taking(way, step, kind))
 
     whole_groups = groups - 1 if last_step >= 2 else groups
 
@@ -525,7 +549,7 @@
     def stage_grads(k):
         if 0 <= k < local:
             gradients(k)
-            if k % 2 and 1 < k < local - 2:
+            if k == 3:
                 trade(1)
 
     def stage_complete(k):
@@ -550,6 +574,8 @@
         if b:
             for k in chunks:
                 pair_left(k)
+        if b == 1:
+            trade(2)
         if b == blocks - 2 and early:
             stage_rows(0)
         if b + 1 < blocks:
@@ -618,7 +644,7 @@
         sem = psent.at[n, 0 if part < pushed else 1]
         copies["p", n, part] = start(remote(
             picked.at[n, :, pl.ds(lane, part_lanes)], out.at[:, there],
-            (sem, precv.at[n, part]), to, feat), condition)
+            (sem, precv.at[n, 0 if part < pushed else 1]), to, feat), condition)
 
     def fill_rows(part):
         count = 4 if part < pushed else 2
@@ -633,8 +659,8 @@
 
     def hand_rows(part, condition):
         if part < pushed:
+            give(part, 2, partner * 2 + 1 - x, inner)
             give(part, 1, partner * 2 + x, inner)
-            give(part, 2, partner * 2 + 1 - x, inner)
         give(part, 0, beside, condition)
 
     def rows_for_slots(part):
@@ -687,8 +713,7 @@
         send_scores(0, sc, True)
 
     if pushed:
-        for group in range(groups):
-            pass_on(1, group, (0,))
+        take_pushed()
         pass_on(1, groups - 1, (1,))
         for part in range(pushed):
             rows_for_slots(part)
@@ -744,12 +769,15 @@
             when(outer, add_more)
 
     def drain():
-        for part in range(quarters):
-            arrives = no(outer) if part < pushed else True
-            when(arrives, copies["p", 0, part].wait_recv)
-        for part in range(pushed):
-            for n in (1, 2):
-                when(outer, copies["p", n, part].wait_recv)
+        def columns(half, first, count):
+            lanes = half * half_lanes + first * part_lanes
+            return out.at[:, pl.ds(pl.multiple_of(lanes, part_lanes), count * part_lanes)]
+
+        await_all(columns(1 - x, pushed, quarters - pushed), precv.at[0, 1])
+        if pushed:
+            await_all(columns(1 - x, 0, pushed), precv.at[0, 0], no(outer))
+            for n, half in ((1, x), (2, 1 - x)):
+                await_all(columns(half, 0, pushed), precv.at[n, 0], outer)
         sum_scores()
         if planes > 1:
             z_sent()
@@ -849,15 +877,16 @@
             vmem(2, 2, feats, score_rows, lanes),
             vmem(2, 2 * feats, score_rows, lanes),
             dma((2 * (local // 2 if local % 2 == 0 else local) + 7,)),
-            dma((2, local)),
+            dma((2, local // 2 if local % 2 == 0 else local)),
             dma((2, local, chips - 1)),
             dma((local,)),
             dma((local,)),
             dma((2,)),
-            dma((2, 2, steps, (local + 1) // 2)),
+            dma((2, local // 2 + 1)),
+            dma((2, steps, (local + 1) // 2)),
             dma((2, quarters)),
             dma((8,)),
-            dma((3, quarters)),
+            dma((3, 2)),
             dma((2,)),
             dma((2,)),
             dma((2, chips - 1)),

time: 59.4 us -> 58 us (0.976)
  Pallas kernels: 57.3 us -> 55.8 us
    pallas_call x1, Pallas kernels: 57.3 us -> 55.8 us  [body(): pl.pallas_call(functools.partial(kernel, (toks, feats, local, chunk, rank...]
where the time goes in v5:
time: 58 us; the launch traced here: 57.9 us
  Pallas kernels  55.8 us (96%)
  local copies, waits for them, and re-layouts  1.39 us (2%)
  between operations  0.64 us (1%)
    pallas_call x1, Pallas kernels, body(): pl.pallas_call(functools.partial(kernel, (toks, feats, local, chunk, rank...  55.8 us
    unnamed x2, local copies, waits for them, and re-layouts  1.39 us

profile of v5, /device:TPU:0, one launch (start us, length us, event | category | flops | bytes accessed | tf_op | source)
XLA Modules:
  0.0 57.9 jit_solution(69534945243311104)
XLA Ops:
  0.6 55.8 %influence.1 = (f32[8,64]{1,0:T(8,128)S(1)}, f32[8,16384]{1,0:T(8,128)S(1)}) custom-call(bf16[1024,2048]{1,0:T(8,128)(2,1)} %refs_0_.1, bf16[1024,7168]{1,0:T(8,128)(2,1)} %refs_1_.1, bf16[2048,256]{1,0:T(8,128)(2,1)} %refs_2_.1, bf16[7168,256]{1,0:T(8,128)(2,1)} %refs_3_.1, f32[256,256]{1,0:T(8,128)} %refs_4_.1, f32[256,256]{1,0:T(8,128)} %refs_5_.1, ...), custom_call_target="tpu_custom_call" | custom-call | tf_op jit(solution)/shard_map/influence/pallas_call | solution.py:835
  56.5 0.6 %copy.13 = f32[8,64]{1,0:T(8,128)} copy(f32[8,64]{1,0:T(8,128)S(1)} %get-tuple-element.2) | data formatting | bytes 4096
  57.1 0.8 %copy.14 = f32[8,16384]{1,0:T(8,128)} copy(f32[8,16384]{1,0:T(8,128)S(1)} %get-tuple-element.3) | data formatting | bytes 1048576

commit v6 on v5

--- a/solution.py
+++ b/solution.py
@@ -549,8 +549,6 @@
     def stage_grads(k):
         if 0 <= k < local:
             gradients(k)
-            if k == 3:
-                trade(1)
 
     def stage_complete(k):
         if 0 <= k < local:

time: 58 us -> 58.4 us (level)
  no operation moved by 1% of the time
where the time goes in v6:
time: 58.4 us; the launch traced here: 58.3 us
  Pallas kernels  56.2 us (96%)
  local copies, waits for them, and re-layouts  1.39 us (2%)
  between operations  0.64 us (1%)
    pallas_call x1, Pallas kernels, body(): pl.pallas_call(functools.partial(kernel, (toks, feats, local, chunk, rank...  56.2 us
    unnamed x2, local copies, waits for them, and re-layouts  1.39 us

profile of v6, /device:TPU:0, one launch (start us, length us, event | category | flops | bytes accessed | tf_op | source)
XLA Modules:
  0.0 58.3 jit_solution(6935932690461970927)
XLA Ops:
  0.6 56.2 %influence.1 = (f32[8,64]{1,0:T(8,128)S(1)}, f32[8,16384]{1,0:T(8,128)S(1)}) custom-call(bf16[1024,2048]{1,0:T(8,128)(2,1)} %refs_0_.1, bf16[1024,7168]{1,0:T(8,128)(2,1)} %refs_1_.1, bf16[2048,256]{1,0:T(8,128)(2,1)} %refs_2_.1, bf16[7168,256]{1,0:T(8,128)(2,1)} %refs_3_.1, f32[256,256]{1,0:T(8,128)} %refs_4_.1, f32[256,256]{1,0:T(8,128)} %refs_5_.1, ...), custom_call_target="tpu_custom_call" | custom-call | tf_op jit(solution)/shard_map/influence/pallas_call | solution.py:833
  56.9 0.6 %copy.13 = f32[8,64]{1,0:T(8,128)} copy(f32[8,64]{1,0:T(8,128)S(1)} %get-tuple-element.2) | data formatting | bytes 4096
  57.5 0.8 %copy.14 = f32[8,16384]{1,0:T(8,128)} copy(f32[8,16384]{1,0:T(8,128)S(1)} %get-tuple-element.3) | data formatting | bytes 1048576
